TPU v7x, 128 devices: a whole 4x4x4 slice. The times are simulated.
128 devices in a mesh: seq: 32 (over z, x_hi, y), mp: 4 (over x_lo, core).
Axes of the slice: x: 4 (x_hi: 2, x_lo: 2; x = x_hi * 2 + x_lo), y: 4, z: 4, core: 2. Of those that a mesh axis runs over, the one named last changes fastest.
Arguments:
- ids: int32 [4096], P('seq'), may hold values from 0 to 3
- hidden_fwd: bfloat16 [4096, 1024], P('seq', 'mp'), may hold values from -8 to 8
- hidden_rc: bfloat16 [4096, 1024], P('seq', 'mp'), may hold values from -8 to 8
- embed: float32 [4, 1024], P(None, 'mp'), may hold values from -4 to 4
- ln1_gain: float32 [1024], replicated, may hold values from 0.1 to 1.9
- ln2_gain: float32 [1024], replicated, may hold values from 0.1 to 1.9
- mixing: float32 [5, 1024], replicated, may hold values from 0 to 1
- w_receptance: bfloat16 [1024, 1024], P(None, 'mp'), may hold values from -0.1875 to 0.1875
- w_key: bfloat16 [1024, 1024], P(None, 'mp'), may hold values from -0.1875 to 0.1875
- w_value: bfloat16 [1024, 1024], P(None, 'mp'), may hold values from -0.1875 to 0.1875
- decay_first_weight: bfloat16 [1024, 64], replicated, may hold values from -0.1875 to 0.1875
- decay_base: float32 [1024], P('mp'), may hold values from -11 to 1
- decay_second_weight: bfloat16 [64, 1024], P(None, 'mp'), may hold values from -0.75 to 0.75
- context_rate_first_weight: bfloat16 [1024, 64], replicated, may hold values from -0.1875 to 0.1875
- iclr_base: float32 [1024], P('mp'), may hold values from -9 to 1
- context_rate_second_weight: bfloat16 [64, 1024], P(None, 'mp'), may hold values from -0.75 to 0.75
- group_gain: float32 [1024], P('mp'), may hold values from 0.1 to 1.9
- w_output: bfloat16 [1024, 1024], P('mp'), may hold values from -0.1875 to 0.1875
- ffn_key: bfloat16 [1024, 4096], P(None, 'mp'), may hold values from -0.1875 to 0.1875
- ffn_value: bfloat16 [4096, 1024], P('mp'), may hold values from -0.09375 to 0.09375
Outputs:
- merged: bfloat16 [4096, 1024], P('seq', 'mp')
Inputs may be any that keep to these rules, and one draw needn't show every extreme that they name: `ids`: bases A, C, G, T are 0, 1, 2, 3; the complement of base c is 3 - c.
All inputs are finite; a program needn't handle non-finite values.
Results may differ from a plain program's by a relative error of at most 0.01.
Values may be sent and summed in bfloat16 or wider, within the bound.
A program may use at most 64 MiB of HBM per device.

v0:
```python
import jax
import jax.numpy as jnp
from jax import lax
from jax.sharding import Mesh
from jax.sharding import PartitionSpec as P

HEAD = 64
BLOCK = 128
SEQ = ("seq_0", "seq_1", "seq_2")


PRECISE = lax.Precision.HIGHEST
DECAY_SCALE = 0.606531
NORM_EPS = 1e-05
GROUP_EPS = 0.00064
UNIT_EPS = 1e-06


def swapped(value, axis, apart):
    mask = 2**apart
    pairs = [(source, source ^ mask) for source in range(lax.axis_size(axis))]
    return lax.ppermute(value, axis, pairs)


def extended(array, sides, width):
    for axis, dim in sides:
        size, length = (lax.axis_size(axis), array.shape[dim])
        up = [(i, (i + 1) % size) for i in range(size - 1)]
        down = [(j, i) for i, j in up]
        last = lax.slice_in_dim(array, length - width, length, axis=dim)
        initial = lax.slice_in_dim(array, 0, width, axis=dim)
        before = lax.ppermute(last, axis, up)
        after = lax.ppermute(initial, axis, down)
        array = jnp.concatenate([before, array, after], axis=dim)
    return array


def nothing_yet(array, identity):
    return jax.tree.map(
        lambda part, zero: jnp.zeros_like(part) + jnp.asarray(zero, part.dtype), array, identity
    )


def prefix_by_axis(array, axes, combine, identity, reverse):
    before = start = nothing_yet(array, identity)
    so_far = array
    for axis in reversed(axes):
        length, index = (lax.axis_size(axis), lax.axis_index(axis))
        pieces = jax.tree.map(lambda part: lax.all_gather(part, axis), so_far)
        inside, so_far = (start, start)
        for k in reversed(range(length)) if reverse else range(length):
            passed = k > index if reverse else k < index
            so_far = combine(so_far, jax.tree.map(lambda part: part[k], pieces))
            inside = jax.tree.map(lambda new, old: jnp.where(passed, new, old), so_far, inside)
        before = combine(inside, before)
    return before


def in_blocks(array, dim, length):
    shape = array.shape
    parts = array.reshape(*shape[:dim], length, shape[dim] // length, *shape[dim + 1 :])
    return jnp.moveaxis(parts, dim, 0)


def sent_and_summed(array, axis, dim):
    parts = in_blocks(array, dim, lax.axis_size(axis))
    arrived = lax.all_to_all(parts, axis, split_axis=0, concat_axis=0, tiled=True)
    return arrived.astype(jnp.float32).sum(axis=0)


def layer_norm(values, gain):
    row_mean = jnp.mean(values, axis=-1, keepdims=True)
    centered = values - row_mean
    spread = jnp.mean(centered * centered, axis=-1, keepdims=True)
    return centered * lax.rsqrt(spread + NORM_EPS) * gain


def project(layer_input, weight):
    flat = layer_input.reshape(-1, layer_input.shape[-1])
    result = jnp.dot(flat, weight, preferred_element_type=jnp.float32)
    return result.reshape(layer_input.shape[:-1] + (weight.shape[1],))


def pairing(left_side, right_side, keep_mask):
    scores = jnp.einsum("lbtc,lbsc->lbts", left_side, right_side, precision=PRECISE)
    return jnp.where(keep_mask, scores, 0.0)


def square_product(left_side, right_side):
    return jnp.einsum("lbts,lbsu->lbtu", left_side, right_side, precision=PRECISE)


def unit_lower_inverse(strict_part):
    length = strict_part.shape[-1]
    power = strict_part
    inverse = jnp.eye(length, dtype=jnp.float32) + power
    reach = 2
    while reach < length:
        power = square_product(power, power)
        inverse = inverse + square_product(inverse, power)
        reach = reach * 2
    return inverse


def state_product(state_in, mapping):
    return jnp.einsum("lvk,lkj->lvj", state_in, mapping, precision=PRECISE)


def compose(earlier_pair, later_pair):
    return (
        state_product(earlier_pair[0], later_pair[0]),
        state_product(earlier_pair[1], later_pair[0]) + later_pair[1],
    )


def block_terms(receptance, key_vec, value_vec, unit_key, iclr_rate, log_decay):
    length = receptance.shape[2]
    width_value = value_vec.shape[3]
    totals = jnp.cumsum(log_decay, axis=2)
    earlier = totals - log_decay
    middle = totals[:, :, length // 2 : length // 2 + 1]
    final_position = totals[:, :, length - 1 : length]
    removal = -unit_key
    insertion = iclr_rate * unit_key
    left_prev = removal * jnp.exp(earlier - middle)
    left_here = receptance * jnp.exp(totals - middle)
    right_insert = insertion * jnp.exp(middle - totals)
    right_key = key_vec * jnp.exp(middle - totals)
    row_ids = lax.broadcasted_iota(jnp.int32, (length, length), 0)
    col_ids = lax.broadcasted_iota(jnp.int32, (length, length), 1)
    strict = row_ids > col_ids
    inclusive = row_ids >= col_ids
    insert_pull = pairing(left_prev, right_insert, strict)
    key_pull = pairing(left_prev, right_key, strict)
    insert_read = pairing(left_here, right_insert, inclusive)
    key_read = pairing(left_here, right_key, inclusive)
    inverse = unit_lower_inverse(insert_pull)
    start_removal = removal * jnp.exp(earlier)
    start_read = receptance * jnp.exp(totals)
    to_end = jnp.exp(final_position - totals)
    tail_insert = insertion * to_end
    tail_key = key_vec * to_end
    value_pull = jnp.einsum("lbts,lbsv->lbtv", key_pull, value_vec, precision=PRECISE)
    solved = jnp.einsum(
        "lbts,lbsv->lbtv",
        inverse,
        jnp.concatenate([value_pull, start_removal], axis=3),
        precision=PRECISE,
    )
    local_pull = solved[..., :width_value]
    start_pull = solved[..., width_value:]
    carried = jnp.einsum("lbst,lbsk->lbtk", inverse, tail_insert, precision=PRECISE)
    local_out = jnp.einsum(
        "lbts,lbsv->lbtv", insert_read, local_pull, precision=PRECISE
    ) + jnp.einsum("lbts,lbsv->lbtv", key_read, value_vec, precision=PRECISE)
    start_map = start_read + jnp.einsum(
        "lbts,lbsk->lbtk", insert_read, start_pull, precision=PRECISE
    )
    key_eye = jnp.eye(unit_key.shape[3], dtype=jnp.float32)
    transition = (
        jnp.einsum("lbtk,lbtj->lbkj", start_removal, carried, precision=PRECISE)
        + key_eye * jnp.exp(final_position)[:, :, 0, :, None]
    )
    local_end = jnp.einsum(
        "lbtv,lbtk->lbvk", local_pull, tail_insert, precision=PRECISE
    ) + jnp.einsum("lbtv,lbtk->lbvk", value_vec, tail_key, precision=PRECISE)
    return (local_out, start_map, transition, local_end)


def through_blocks(carry_pair, pieces):
    transition, local_end = pieces
    advanced = (
        state_product(carry_pair[0], transition),
        state_product(carry_pair[1], transition) + local_end,
    )
    return (advanced, carry_pair)


def on_device(
    ids,
    hidden_fwd,
    hidden_rc,
    embed,
    ln1_gain,
    ln2_gain,
    mixing,
    w_receptance,
    w_key,
    w_value,
    decay_first_weight,
    decay_base,
    decay_second_weight,
    context_rate_first_weight,
    iclr_base,
    context_rate_second_weight,
    group_gain,
    w_output,
    ffn_key,
    ffn_value,
):
    seq_rows = ids.shape[0]
    local_width = hidden_fwd.shape[1]
    local_heads = local_width // HEAD
    lanes_total = 4 * local_heads
    half_lanes = 2 * local_heads
    seq_count = lax.axis_size(SEQ)
    mirrored_ids = ids
    for bit_index in range(seq_count.bit_length() - 1):
        mirrored_ids = swapped(mirrored_ids, SEQ, bit_index)
    letters = jnp.arange(4, dtype=jnp.int32)
    onehot_fwd = (ids[:, None] == letters[None, :]).astype(jnp.float32)
    onehot_rc = ((3 - mirrored_ids[::-1])[:, None] == letters[None, :]).astype(jnp.float32)
    strands = jnp.stack(
        [
            hidden_fwd.astype(jnp.float32) + jnp.dot(onehot_fwd, embed, precision=PRECISE),
            hidden_rc.astype(jnp.float32) + jnp.dot(onehot_rc, embed, precision=PRECISE),
        ]
    ).astype(jnp.bfloat16)
    padded = extended(strands, ((SEQ, 1),), 1)
    whole_rows = lax.all_gather(padded, "mp", axis=2, tiled=True)
    normed = layer_norm(whole_rows.astype(jnp.float32), ln1_gain)
    center = normed[None, :, 1:-1]
    neighbours = jnp.stack([normed[:, :-2], normed[:, 2:]])

    def mixed_input(mix_index):
        return (center + (neighbours - center) * mixing[mix_index]).astype(jnp.bfloat16)

    receptance = project(mixed_input(0), w_receptance)
    key_vec = project(mixed_input(1), w_key)
    value_vec = project(mixed_input(2), w_value)
    decay_low = jnp.tanh(project(mixed_input(3), decay_first_weight)).astype(jnp.bfloat16)
    log_decay = -DECAY_SCALE * jax.nn.sigmoid(decay_base + project(decay_low, decay_second_weight))
    iclr_low = project(mixed_input(4), context_rate_first_weight).astype(jnp.bfloat16)
    iclr_rate = jax.nn.sigmoid(iclr_base + project(iclr_low, context_rate_second_weight))

    def heads_first(array):
        lanes = array.reshape(2, 2, seq_rows, local_heads, HEAD)
        lanes = jnp.stack([lanes[0], lanes[1][:, ::-1]])
        lanes = jnp.transpose(lanes, (0, 1, 3, 2, 4))
        return lanes.reshape(lanes_total, seq_rows // BLOCK, BLOCK, HEAD)

    key_lanes = heads_first(key_vec)
    unit_key = key_lanes * lax.rsqrt(
        jnp.sum(key_lanes * key_lanes, axis=-1, keepdims=True) + UNIT_EPS
    )
    local_out, start_map, transition, local_end = block_terms(
        heads_first(receptance),
        key_lanes,
        heads_first(value_vec),
        unit_key,
        heads_first(iclr_rate),
        heads_first(log_decay),
    )
    identity = jnp.broadcast_to(jnp.eye(HEAD, dtype=jnp.float32), (lanes_total, HEAD, HEAD))
    empty_state = jnp.zeros((lanes_total, HEAD, HEAD), jnp.float32)
    (device_map, device_end), (prefix_maps, prefix_states) = lax.scan(
        through_blocks,
        (identity, empty_state),
        (jnp.moveaxis(transition, 1, 0), jnp.moveaxis(local_end, 1, 0)),
    )
    _, from_below = prefix_by_axis(
        (device_map[:half_lanes], device_end[:half_lanes]),
        SEQ,
        compose,
        (identity[:half_lanes], empty_state[:half_lanes]),
        False,
    )
    _, from_above = prefix_by_axis(
        (device_map[half_lanes:], device_end[half_lanes:]),
        SEQ,
        compose,
        (identity[half_lanes:], empty_state[half_lanes:]),
        True,
    )
    incoming = jnp.concatenate([from_below, from_above])
    block_starts = jnp.einsum("lvk,nlkj->lnvj", incoming, prefix_maps, precision=PRECISE)
    block_starts = block_starts + jnp.moveaxis(prefix_states, 0, 1)
    wkv_lanes = local_out + jnp.einsum(
        "lbtk,lbvk->lbtv", start_map, block_starts, precision=PRECISE
    )
    wkv_out = wkv_lanes.reshape(2, 2, local_heads, seq_rows, HEAD)
    wkv_out = jnp.stack([wkv_out[0], wkv_out[1][:, :, ::-1]])
    head_mean = jnp.mean(wkv_out, axis=-1, keepdims=True)
    centered = wkv_out - head_mean
    head_spread = jnp.mean(centered * centered, axis=-1, keepdims=True)
    head_gain = group_gain.reshape(local_heads, HEAD)[None, None, :, None, :]
    grouped = centered * lax.rsqrt(head_spread + GROUP_EPS) * head_gain
    joined = jnp.transpose(grouped[0] + grouped[1], (0, 2, 1, 3)).reshape(2, seq_rows, local_width)
    joined = joined.astype(jnp.bfloat16)
    attention_part = project(joined, w_output)
    attention_whole = lax.psum(attention_part, "mp")
    residual_whole = whole_rows[:, 1:-1].astype(jnp.float32) + attention_whole
    ffn_in = layer_norm(residual_whole, ln2_gain).astype(jnp.bfloat16)
    pre_active = project(ffn_in, ffn_key)
    residual = lax.dynamic_slice_in_dim(
        residual_whole, lax.axis_index("mp") * local_width, local_width, 2
    )
    activated = jnp.square(jax.nn.relu(pre_active)).astype(jnp.bfloat16)
    ffn_local = sent_and_summed(project(activated, ffn_value).astype(jnp.bfloat16), "mp", 2)
    strand_out = residual + ffn_local
    rc_final = strand_out[1].astype(jnp.bfloat16)
    arrived = rc_final
    for bit_index in range(seq_count.bit_length() - 1):
        arrived = swapped(arrived, SEQ, bit_index)
    return (strand_out[0] + arrived[::-1].astype(jnp.float32)).astype(jnp.bfloat16)


def solution(mesh):
    split = Mesh(mesh.devices.reshape(4, 2, 4, mesh.shape["mp"]), ("seq_0", "seq_1", "seq_2", "mp"))
    placed = (
        P(SEQ),
        P(SEQ, "mp"),
        P(SEQ, "mp"),
        P(None, "mp"),
        P(),
        P(),
        P(),
        P(None, "mp"),
        P(None, "mp"),
        P(None, "mp"),
        P(),
        P("mp"),
        P(None, "mp"),
        P(),
        P("mp"),
        P(None, "mp"),
        P("mp"),
        P("mp", None),
        P(None, "mp"),
        P("mp", None),
    )
    return jax.shard_map(
        on_device, mesh=split, in_specs=placed, out_specs=P(SEQ, "mp"), check_vma=False
    )
```

profile of v0, /device:TPU:0, one launch (start us, length us, event | category | flops | bytes accessed | tf_op | source)
XLA Modules:
  0.0 416.7 jit_solution(10083063597854261989)
XLA Ops:
  11.0 3.0 collective-permute-start.1
  16.1 3.0 collective-permute-start.2
  24.8 3.9 collective-permute-start.4
  36.9 2.8 collective-permute-done.6
  39.7 7.3 %all_gather.75 = bf16[2,130,1024]{2,1,0:T(8,128)(2,1)S(1)} all-gather(bf16[2,130,256]{2,1,0:T(8,128)(2,1)S(1)} %pad_maximum_fusion.4), channel_id=1, replica_groups=mesh['seq_0'=4,'seq_1'=2,'seq_2'=4,'mp'=4] {'mp'}, dimensions={2}, use_global_device_ids=true | all-gather | bytes 665600 | tf_op jit(solution)/shard_map/all_gather | solution.py:220
  51.2 3.5 fusion.29
  56.8 3.5 fusion.31
  71.2 4.0 fusion.2
  96.3 2.8 convolution_select_fusion.1
  99.2 2.8 convolution_select_fusion.3
  102.0 2.8 convolution_select_fusion
  139.6 20.3 %all-gather = f32[32,64,64]{2,1,0:T(8,128)S(1)} all-gather(f32[8,64,64]{2,1,0:T(8,128)S(1)} %get-tuple-element.51), channel_id=2, replica_groups=mesh['seq_0'=4,'seq_1'=2,'seq_2'=4,'mp'=4] {'seq_2'}, dimensions={0}, use_global_device_ids=true | all-gather | bytes 655360 | tf_op jit(solution)/shard_map/all_gather | solution.py:49
  161.4 9.3 %all-gather.1 = f32[16,64,64]{2,1,0:T(8,128)S(1)} all-gather(f32[8,64,64]{2,1,0:T(8,128)S(1)} %fusion.146), channel_id=3, replica_groups=mesh['seq_0'=4,'seq_1'=2,'seq_2'=4,'mp'=4] {'seq_1'}, dimensions={0}, use_global_device_ids=true | all-gather | bytes 393216 | tf_op jit(solution)/shard_map/all_gather | solution.py:49
  171.5 16.1 %all-gather.2 = f32[32,64,64]{2,1,0:T(8,128)S(1)} all-gather(f32[8,64,64]{2,1,0:T(8,128)S(1)} %fusion.140), channel_id=4, replica_groups=mesh['seq_0'=4,'seq_1'=2,'seq_2'=4,'mp'=4] {'seq_0'}, dimensions={0}, use_global_device_ids=true | all-gather | bytes 655360 | tf_op jit(solution)/shard_map/all_gather | solution.py:49
  187.6 13.8 %all-gather.3 = f32[32,64,64]{2,1,0:T(8,128)S(1)} all-gather(f32[8,64,64]{2,1,0:T(8,128)S(1)} %get-tuple-element.53), channel_id=5, replica_groups=mesh['seq_0'=4,'seq_1'=2,'seq_2'=4,'mp'=4] {'seq_2'}, dimensions={0}, use_global_device_ids=true | all-gather | bytes 655360 | tf_op jit(solution)/shard_map/all_gather | solution.py:49
  203.0 8.8 %all-gather.4 = f32[16,64,64]{2,1,0:T(8,128)S(1)} all-gather(f32[8,64,64]{2,1,0:T(8,128)S(1)} %convolution_add_fusion.28), channel_id=6, replica_groups=mesh['seq_0'=4,'seq_1'=2,'seq_2'=4,'mp'=4] {'seq_1'}, dimensions={0}, use_global_device_ids=true | all-gather | bytes 393216 | tf_op jit(solution)/shard_map/all_gather | solution.py:49
  213.8 13.8 %all-gather.5 = f32[32,64,64]{2,1,0:T(8,128)S(1)} all-gather(f32[8,64,64]{2,1,0:T(8,128)S(1)} %convolution_add_fusion.27), channel_id=7, replica_groups=mesh['seq_0'=4,'seq_1'=2,'seq_2'=4,'mp'=4] {'seq_0'}, dimensions={0}, use_global_device_ids=true | all-gather | bytes 655360 | tf_op jit(solution)/shard_map/all_gather | solution.py:49
  227.6 13.8 %all-gather.6 = f32[32,64,64]{2,1,0:T(8,128)S(1)} all-gather(f32[8,64,64]{2,1,0:T(8,128)S(1)} %get-tuple-element.52), channel_id=8, replica_groups=mesh['seq_0'=4,'seq_1'=2,'seq_2'=4,'mp'=4] {'seq_2'}, dimensions={0}, use_global_device_ids=true | all-gather | bytes 655360 | tf_op jit(solution)/shard_map/all_gather | solution.py:49
  243.0 8.5 %all-gather.7 = f32[16,64,64]{2,1,0:T(8,128)S(1)} all-gather(f32[8,64,64]{2,1,0:T(8,128)S(1)} %fusion.128), channel_id=9, replica_groups=mesh['seq_0'=4,'seq_1'=2,'seq_2'=4,'mp'=4] {'seq_1'}, dimensions={0}, use_global_device_ids=true | all-gather | bytes 393216 | tf_op jit(solution)/shard_map/all_gather | solution.py:49
  252.3 13.8 %all-gather.8 = f32[32,64,64]{2,1,0:T(8,128)S(1)} all-gather(f32[8,64,64]{2,1,0:T(8,128)S(1)} %fusion.122), channel_id=10, replica_groups=mesh['seq_0'=4,'seq_1'=2,'seq_2'=4,'mp'=4] {'seq_0'}, dimensions={0}, use_global_device_ids=true | all-gather | bytes 655360 | tf_op jit(solution)/shard_map/all_gather | solution.py:49
  266.2 13.8 %all-gather.9 = f32[32,64,64]{2,1,0:T(8,128)S(1)} all-gather(f32[8,64,64]{2,1,0:T(8,128)S(1)} %get-tuple-element.54), channel_id=11, replica_groups=mesh['seq_0'=4,'seq_1'=2,'seq_2'=4,'mp'=4] {'seq_2'}, dimensions={0}, use_global_device_ids=true | all-gather | bytes 655360 | tf_op jit(solution)/shard_map/all_gather | solution.py:49
  281.6 8.5 %all-gather.10 = f32[16,64,64]{2,1,0:T(8,128)S(1)} all-gather(f32[8,64,64]{2,1,0:T(8,128)S(1)} %convolution_add_fusion.17), channel_id=12, replica_groups=mesh['seq_0'=4,'seq_1'=2,'seq_2'=4,'mp'=4] {'seq_1'}, dimensions={0}, use_global_device_ids=true | all-gather | bytes 393216 | tf_op jit(solution)/shard_map/all_gather | solution.py:49
  292.1 14.1 %all-gather.11 = f32[32,64,64]{2,1,0:T(8,128)S(1)} all-gather(f32[8,64,64]{2,1,0:T(8,128)S(1)} %convolution_add_fusion.16), channel_id=13, replica_groups=mesh['seq_0'=4,'seq_1'=2,'seq_2'=4,'mp'=4] {'seq_0'}, dimensions={0}, use_global_device_ids=true | all-gather | bytes 655360 | tf_op jit(solution)/shard_map/all_gather | solution.py:49
  322.0 40.2 %all-reduce.2.cloned.1.call-done = f32[2,128,1024]{2,1,0:T(8,128)} async-done(((f32[2,128,1024]{2,1,0:T(8,128)}), f32[2,128,1024]{2,1,0:T(8,128)}) %all-reduce.2.cloned.1.call-update) | async-done | bytes 1048592 | tf_op jit(solution)/shard_map/psum | solution.py:291
  365.0 3.2 fusion.15
  369.1 3.5 all-to-all-start
  372.5 8.8 %all-to-all-done = bf16[4,2,128,256]{3,2,1,0:T(8,128)(2,1)S(1)} async-done(((bf16[4,2,128,256]{3,2,1,0:T(8,128)(2,1)}), bf16[4,2,128,256]{3,2,1,0:T(8,128)(2,1)S(1)}, u32[]{:S(2)}, u32[]{:S(2)}) %all-to-all-start) | async-done | bytes 524320 | tf_op jit(solution)/shard_map/all_to_all | solution.py:67
  386.8 3.0 collective-permute-start.8
  392.5 2.9 collective-permute-start.9
  395.4 2.9 collective-permute-done.9
  399.8 3.1 collective-permute-done.10
  405.7 3.0 collective-permute-done.11
  (256 shorter events, 136.7 us)
Async XLA Ops:
  6.5 358.4 %copy-start = (bf16[1024,1024]{1,0:T(8,128)(2,1)S(1)}, bf16[1024,1024]{1,0:T(8,128)(2,1)}, u32[]{:S(2)}) copy-start(bf16[1024,1024]{1,0:T(8,128)(2,1)} %param.39) | copy-start | bytes 6291460
  6.5 41.0 %copy-start.39 = (f32[1024]{0:T(1024)S(1)}, f32[1024]{0:T(1024)}, u32[]{:S(2)}) copy-start(f32[1024]{0:T(1024)} %param.24) | copy-start | bytes 12292
  6.5 355.7 %all-reduce.2.cloned.1.call-start = ((), (), s32[]{:S(2)}) async-start(), calls=%async_computation.1 | async-start | bytes 2097152 | tf_op jit(solution)/shard_map/psum | solution.py:291
  6.5 4.4 %collective-permute-start = (s32[128]{0:T(128)}, s32[128]{0:T(128)S(1)}, u32[]{:S(2)}, u32[]{:S(2)}) collective-permute-start(s32[128]{0:T(128)} %param.20), channel_id=1, source_target_pairs={{0,4},{4,0},{8,12},{12,8},{16,20},{20,16},{24,28},{28,24},{32,36},... | collective-permute-start | bytes 1544 | tf_op jit(solution)/shard_map/ppermute | solution.py:22
  11.0 5.2 %collective-permute-start.1 = (s32[128]{0:T(128)S(1)}, s32[128]{0:T(128)S(1)}, u32[]{:S(2)}, u32[]{:S(2)}) collective-permute-start(s32[128]{0:T(128)S(1)} %collective-permute-done), channel_id=1, source_target_pairs={{0,8},{4,12},{8,0},{12,4},{16,24},{20,28},{24,16},{28,20},{32,40},... | collective-permute-start | bytes 1544 | tf_op jit(solution)/shard_map/ppermute | solution.py:22
  16.1 5.1 %collective-permute-start.2 = (s32[128]{0:T(128)S(1)}, s32[128]{0:T(128)S(1)}, u32[]{:S(2)}, u32[]{:S(2)}) collective-permute-start(s32[128]{0:T(128)S(1)} %collective-permute-done.1), channel_id=1, source_target_pairs={{0,16},{4,20},{8,24},{12,28},{16,0},{20,4},{24,8},{28,12},{32,48},... | collective-permute-start | bytes 1544 | tf_op jit(solution)/shard_map/ppermute | solution.py:22
  21.2 3.6 collective-permute-start.3
  24.8 5.4 %collective-permute-start.4 = (s32[128]{0:T(128)S(1)}, s32[128]{0:T(128)S(1)}, u32[]{:S(2)}, u32[]{:S(2)}) collective-permute-start(s32[128]{0:T(128)S(1)} %collective-permute-done.3), channel_id=1, source_target_pairs={{0,64},{4,68},{8,72},{12,76},{16,80},{20,84},{24,88},{28,92},{32,9... | collective-permute-start | bytes 1544 | tf_op jit(solution)/shard_map/ppermute | solution.py:22
  31.4 5.5 %collective-permute-start.5 = (bf16[2,1,256]{2,1,0:T(2,128)(2,1)S(1)}, bf16[2,1,256]{2,1,0:T(2,128)(2,1)S(1)}, u32[]{:S(2)}, u32[]{:S(2)}) collective-permute-start(bf16[2,1,256]{2,1,0:T(2,128)(2,1)S(1)} %get-tuple-element.65), channel_id=1, source_target_pairs={{0,4},{4,8},{8,12},{12,16},{16,20},{20,24},{24,28},{28,32},{32,36}... | collective-permute-start | bytes 3080 | tf_op jit(solution)/shard_map/ppermute | solution.py:32
  34.2 5.5 %collective-permute-start.6 = (bf16[2,1,256]{2,1,0:T(2,128)(2,1)S(1)}, bf16[2,1,256]{2,1,0:T(2,128)(2,1)S(1)}, u32[]{:S(2)}, u32[]{:S(2)}) collective-permute-start(bf16[2,1,256]{2,1,0:T(2,128)(2,1)S(1)} %get-tuple-element.66), channel_id=1, source_target_pairs={{4,0},{8,4},{12,8},{16,12},{20,16},{24,20},{28,24},{32,28},{36,32}... | collective-permute-start | bytes 3080 | tf_op jit(solution)/shard_map/ppermute | solution.py:33
  65.2 2.7 copy-start.4
  66.6 4.6 %copy-start.35 = (f32[1,1024]{1,0:T(1,128)S(1)}, f32[1,1024]{1,0:T(1,128)}, u32[]{:S(2)}) copy-start(f32[1,1024]{1,0:T(1,128)} %get-tuple-element.67) | copy-start | bytes 12292
  66.6 4.6 %copy-start.36 = (f32[1,1024]{1,0:T(1,128)S(1)}, f32[1,1024]{1,0:T(1,128)}, u32[]{:S(2)}) copy-start(f32[1,1024]{1,0:T(1,128)} %get-tuple-element.70) | copy-start | bytes 12292
  66.6 4.6 %copy-start.37 = (f32[1,1024]{1,0:T(1,128)S(1)}, f32[1,1024]{1,0:T(1,128)}, u32[]{:S(2)}) copy-start(f32[1,1024]{1,0:T(1,128)} %get-tuple-element.71) | copy-start | bytes 12292
  71.2 4.0 copy-start.26
  81.9 2.8 copy-start.18
  81.9 2.8 copy-start.27
  94.5 25.0 %copy-start.8 = (f32[16,128,64]{1,2,0:T(8,128)}, f32[16,128,64]{1,2,0:T(8,128)S(1)}, u32[]{:S(2)}) copy-start(f32[16,128,64]{1,2,0:T(8,128)S(1)} %get-tuple-element.35) | copy-start | bytes 1572868
  120.5 4.0 copy-start.17
  120.5 4.0 copy-start.28
  126.9 5.7 %copy-start.31 = (f32[2,2,4,128]{3,2,1,0:T(4,128)S(1)}, f32[2,2,4,128]{3,2,1,0:T(4,128)}, u32[]{:S(2)}) copy-start(f32[2,2,4,128]{3,2,1,0:T(4,128)} %fusion.215) | copy-start | bytes 24580
  135.0 3.3 copy-start.22
  290.9 15.4 %copy-start.3 = (f32[16,128,128]{2,1,0:T(8,128)S(1)}, f32[16,128,128]{2,1,0:T(8,128)}, u32[]{:S(2)}) copy-start(f32[16,128,128]{2,1,0:T(8,128)} %convolution_select_fusion.3) | copy-start | bytes 3145732
  291.7 16.6 %copy-start.11 = (f32[2,2,4,128,64]{3,4,2,1,0:T(8,128)S(1)}, f32[2,2,4,128,64]{3,4,2,1,0:T(8,128)}, u32[]{:S(2)}) copy-start(f32[2,2,4,128,64]{3,4,2,1,0:T(8,128)} %copy-done.10) | copy-start | bytes 1572868
  314.8 2.5 copy-start.15
  322.0 42.9 %copy-start.42 = (f32[1024]{0:T(1024)S(1)}, f32[1024]{0:T(1024)}, u32[]{:S(2)}) copy-start(f32[1024]{0:T(1024)} %param.25) | copy-start | bytes 12292
  369.1 12.3 %all-to-all-start = ((bf16[4,2,128,256]{3,2,1,0:T(8,128)(2,1)}), bf16[4,2,128,256]{3,2,1,0:T(8,128)(2,1)S(1)}, u32[]{:S(2)}, u32[]{:S(2)}) async-start(bf16[4,2,128,256]{3,2,1,0:T(8,128)(2,1)} %bitcast.305), calls=%async_computation | async-start | bytes 1048576 | tf_op jit(solution)/shard_map/all_to_all | solution.py:67
  382.4 4.3 %collective-permute-start.7 = (bf16[128,256]{1,0:T(8,128)(2,1)S(1)}, bf16[128,256]{1,0:T(8,128)(2,1)S(1)}, u32[]{:S(2)}, u32[]{:S(2)}) collective-permute-start(bf16[128,256]{1,0:T(8,128)(2,1)S(1)} %fusion.208), channel_id=1, source_target_pairs={{0,4},{4,0},{8,12},{12,8},{16,20},{20,16},{24,28},{28,24},{32,36},... | collective-permute-start | bytes 196616 | tf_op jit(solution)/shard_map/ppermute | solution.py:22
  386.8 5.8 %collective-permute-start.8 = (bf16[128,256]{1,0:T(8,128)(2,1)S(1)}, bf16[128,256]{1,0:T(8,128)(2,1)S(1)}, u32[]{:S(2)}, u32[]{:S(2)}) collective-permute-start(bf16[128,256]{1,0:T(8,128)(2,1)S(1)} %collective-permute-done.7), channel_id=1, source_target_pairs={{0,8},{4,12},{8,0},{12,4},{16,24},{20,28},{24,16},{28,20},{32,40},... | collective-permute-start | bytes 196616 | tf_op jit(solution)/shard_map/ppermute | solution.py:22
  392.5 5.8 %collective-permute-start.9 = (bf16[128,256]{1,0:T(8,128)(2,1)S(1)}, bf16[128,256]{1,0:T(8,128)(2,1)S(1)}, u32[]{:S(2)}, u32[]{:S(2)}) collective-permute-start(bf16[128,256]{1,0:T(8,128)(2,1)S(1)} %collective-permute-done.8), channel_id=1, source_target_pairs={{0,16},{4,20},{8,24},{12,28},{16,0},{20,4},{24,8},{28,12},{32,48},... | collective-permute-start | bytes 196616 | tf_op jit(solution)/shard_map/ppermute | solution.py:22
  398.3 4.7 %collective-permute-start.10 = (bf16[128,256]{1,0:T(8,128)(2,1)S(1)}, bf16[128,256]{1,0:T(8,128)(2,1)S(1)}, u32[]{:S(2)}, u32[]{:S(2)}) collective-permute-start(bf16[128,256]{1,0:T(8,128)(2,1)S(1)} %collective-permute-done.9), channel_id=1, source_target_pairs={{0,32},{4,36},{8,40},{12,44},{16,48},{20,52},{24,56},{28,60},{32,0... | collective-permute-start | bytes 196616 | tf_op jit(solution)/shard_map/ppermute | solution.py:22
  402.9 5.8 %collective-permute-start.11 = (bf16[128,256]{1,0:T(8,128)(2,1)S(1)}, bf16[128,256]{1,0:T(8,128)(2,1)S(1)}, u32[]{:S(2)}, u32[]{:S(2)}) collective-permute-start(bf16[128,256]{1,0:T(8,128)(2,1)S(1)} %collective-permute-done.10), channel_id=1, source_target_pairs={{0,64},{4,68},{8,72},{12,76},{16,80},{20,84},{24,88},{28,92},{32,9... | collective-permute-start | bytes 196616 | tf_op jit(solution)/shard_map/ppermute | solution.py:22
  (26 other events, 40.9 us)
Sparse Core Ops, SparseCore 0:
  322.1 40.0 all-reduce.1
where the time goes:
time: 425 us; the launch traced here: 417 us
  blocking collectives  162 us (38%)
  matrix products  75.8 us (18%)
  waiting for transfers between devices  73.1 us (17%)
  local copies, waits for them, and re-layouts  37.3 us (9%)
  starting transfers between devices  32.9 us (8%)
  other arithmetic  20.3 us (5%)
  between operations  15.2 us (4%)
    all_gather x12, blocking collectives, prefix_by_axis(): pieces = jax.tree.map(lambda part: lax.all_gather(part, axis), so_far)  155 us
    psum x1, waiting for transfers between devices, on_device(): attention_whole = lax.psum(attention_part, 'mp')  40.2 us
    ppermute x10, starting transfers between devices, swapped(): return lax.ppermute(value, axis, pairs)  25.3 us
    ppermute x10, waiting for transfers between devices, swapped(): return lax.ppermute(value, axis, pairs)  21.3 us
    dot_general x44, matrix products, state_product(): return jnp.einsum('lvk,lkj->lvj', state_in, mapping, precision=PRECISE)  19 us
    slice x18, local copies, waits for them, and re-layouts, heads_first(): lanes = jnp.stack([lanes[0], lanes[1][:, ::-1]])  14.9 us
    dot_general x12, matrix products, square_product(): jnp.einsum('lbts,lbsu->lbtu', left_side, right_side, precision=PRECISE)  14.5 us
    dot_general x7, matrix products, project(): result = jnp.dot(flat, weight, preferred_element_type=jnp.float32)  12.8 us
  transfers between devices with their start and end apart: 14, of which 12 were waited for; matrix products, arithmetic and copies ran while one was open for 1% of the time, Pallas kernels for 0%

commit v1 on v0

v1 whole, which is shorter than its diff:
```python
import functools

import jax
import jax.numpy as jnp
from jax import lax
from jax.experimental import pallas as pl
from jax.experimental.pallas import tpu as pltpu
from jax.sharding import PartitionSpec as P

F32, BF16 = jnp.float32, jnp.bfloat16
HEAD = 64
ROWS = 128
PAIR = 128
LEVELS = 7
DECAY_SCALE = 0.606531
NORM_EPS = 1e-05
GROUP_EPS = 0.00064
UNIT_EPS = 1e-06
MESH = pl.DeviceIdType.MESH


def dot(a, b):
    return lax.dot_general(a, b, (((1,), (0,)), ((), ())), preferred_element_type=F32)


def dot_t(a, b):
    return lax.dot_general(a, b, (((1,), (1,)), ((), ())), preferred_element_type=F32)


def t_dot(a, b):
    return lax.dot_general(a, b, (((0,), (0,)), ((), ())), preferred_element_type=F32)


def halves(value):
    high = value.astype(BF16)
    return high, (value - high.astype(F32)).astype(BF16)


def iota2(shape, dim):
    return lax.broadcasted_iota(jnp.int32, shape, dim)


def left_half(shape):
    return iota2(shape, 1) % PAIR < HEAD


def layer_norm(values, gain):
    centered = values - jnp.mean(values, axis=-1, keepdims=True)
    spread = jnp.mean(centered * centered, axis=-1, keepdims=True)
    return centered * lax.rsqrt(spread + NORM_EPS) * gain


def masks_into(masks):
    row, col = iota2((ROWS, ROWS), 0), iota2((ROWS, ROWS), 1)
    for level in range(LEVELS):
        size = 1 << level
        same = row // (2 * size) == col // (2 * size)
        row_odd, col_odd = (row // size) % 2, (col // size) % 2
        masks[0, level] = jnp.where(same & (row_odd > col_odd), 1.0, 0.0).astype(BF16)
        masks[1, level] = jnp.where(same & (row_odd < col_odd), 1.0, 0.0).astype(BF16)


def two_heads(value):
    left = left_half(value.shape)
    zero = jnp.zeros_like(value)
    return jnp.concatenate([jnp.where(left, value, zero), jnp.where(left, zero, value)], axis=0)


def packed(value, head):
    half = value.shape[0] // 2
    upper, lower = value[:half], value[half:]
    left = left_half(upper.shape)
    if head == 0:
        return jnp.where(left, upper, pltpu.roll(lower, HEAD, 1))
    return jnp.where(left, pltpu.roll(upper, HEAD, 1), lower)


def unpacked(value):
    return jnp.concatenate([value, pltpu.roll(value, HEAD, 1)], axis=0)


def strand_rows(b, x_tile, idm, embf, st):
    for tile in range(8):
        slot, lanes = tile // 2, pl.ds((tile % 2) * PAIR, PAIR)
        added = embf[slot, 3:4, lanes]
        for letter in range(3):
            added = jnp.where(idm == float(letter), embf[slot, letter : letter + 1, lanes], added)
        st[b, :, tile * PAIR : (tile + 1) * PAIR] = (x_tile(tile) + added).astype(BF16)


def edge_row(piece, index, letter_of, embf, gain, keep):
    row = jnp.concatenate([piece[s].astype(F32)[index : index + 1] for s in range(4)], axis=1)
    letter = jnp.broadcast_to(letter_of, row.shape)
    emb = [jnp.concatenate([embf[s, c : c + 1] for s in range(4)], axis=1) for c in range(4)]
    added = emb[3]
    for c in range(3):
        added = jnp.where(letter == float(c), emb[c], added)
    row = (row + added).astype(BF16).astype(F32)
    return layer_norm(row, gain) * keep


def normed_and_mixed(b, st, nrm, mx, gain, mix):
    for chunk in range(4):
        rows = pl.ds(chunk * 32, 32)
        nrm[8 + chunk * 32 : 40 + chunk * 32] = layer_norm(st[b, rows].astype(F32), gain)
    for chunk in range(8):
        at = chunk * 16
        center = nrm[8 + at : 24 + at]
        before = nrm[7 + at : 23 + at] - center
        after = nrm[9 + at : 25 + at] - center
        for index in range(5):
            weight = mix[index : index + 1, :]
            mx[index, at : at + 16] = (center + before * weight).astype(BF16)
            mx[index, ROWS + at : ROWS + at + 16] = (center + after * weight).astype(BF16)


def projected(mx, wr, wk, wv, dfw, dbase, dsw, cfw, ibase, csw, proj):
    def keep(index, value):
        for beta in range(2):
            for q in range(2):
                proj[index, beta, q] = value[
                    beta * ROWS : (beta + 1) * ROWS, q * PAIR : (q + 1) * PAIR
                ]

    keep(0, dot(mx[0], wr[...]))
    key = dot(mx[1], wk[...])
    keep(1, key)
    keep(2, dot(mx[2], wv[...]))
    width = 2 * PAIR
    same_head = iota2((width, width), 0) // HEAD == iota2((width, width), 1) // HEAD
    ones = jnp.where(same_head, 1.0, 0.0).astype(BF16)
    high, low = halves(key * key)
    square = dot(high, ones) + dot(low, ones)
    keep(3, key * lax.rsqrt(square + UNIT_EPS))
    low_iclr = dot(mx[4], cfw[...]).astype(BF16)
    keep(4, jax.nn.sigmoid(ibase[...] + dot(low_iclr, csw[...])))
    low_decay = jnp.tanh(dot(mx[3], dfw[...])).astype(BF16)
    log_decay = -DECAY_SCALE * jax.nn.sigmoid(dbase[...] + dot(low_decay, dsw[...]))
    keep(5, log_decay)
    row, col = iota2((ROWS, ROWS), 0), iota2((ROWS, ROWS), 1)
    totals = []
    for beta in range(2):
        passed = (row >= col) if beta == 0 else (row <= col)
        ones = jnp.where(passed, 1.0, 0.0).astype(BF16)
        high, low = halves(log_decay[beta * ROWS : (beta + 1) * ROWS])
        totals.append(dot(ones, high) + dot(ones, low))
    keep(6, jnp.concatenate(totals, axis=0))


def block_terms(b, q, proj, masks, msg, aik, uw, vv, srd):
    row, col = iota2((ROWS, ROWS), 0), iota2((ROWS, ROWS), 1)
    eye = jnp.where(row == col, 1.0, 0.0)
    for beta in range(2):
        pair = (beta * 2 + b) * 2 + q
        receptance, key, value, unit, iclr, log_decay, total = [
            proj[i, beta, q] for i in range(7)
        ]
        middle = total[64:65] if beta == 0 else total[63:64]
        final = total[127:128] if beta == 0 else total[0:1]
        scale_here = jnp.exp(total - middle)
        scale_right = jnp.exp(middle - total)
        left_prev = -unit * jnp.exp(total - log_decay - middle)
        left_here = receptance * scale_here
        right_insert = iclr * unit * scale_right
        right_key = key * scale_right
        from_start = jnp.exp(middle)
        to_end = jnp.exp(final - middle)
        left = jnp.concatenate(
            [two_heads(left_prev.astype(BF16)), two_heads(left_here.astype(BF16))], axis=0
        )
        right = jnp.concatenate([right_insert, right_key], axis=0).astype(BF16)
        scores = dot_t(left, right)
        strict = (row > col) if beta == 0 else (row < col)
        inclusive = (row >= col) if beta == 0 else (row <= col)
        inverses = []
        for head in range(2):
            lower = jnp.where(strict, scores[head * ROWS : (head + 1) * ROWS, :ROWS], 0.0)
            lower = lower.astype(BF16)
            inverse = eye + (lower * masks[beta, 0]).astype(F32)
            for level in range(1, LEVELS):
                narrow = inverse.astype(BF16)
                step = dot(narrow, lower * masks[beta, level]).astype(BF16)
                inverse = inverse + dot(step, narrow)
            inverses.append(inverse.astype(BF16))
            at = 2 * ROWS + head * ROWS
            aik[pair, :, head * ROWS : (head + 1) * ROWS] = jnp.where(
                inclusive, scores[at : at + ROWS, :ROWS], 0.0
            ).astype(BF16)
            aik[pair, :, (2 + head) * ROWS : (3 + head) * ROWS] = jnp.where(
                inclusive, scores[at : at + ROWS, ROWS:], 0.0
            ).astype(BF16)
        value = value.astype(BF16)
        vv[pair] = value
        srd[pair] = left_here * from_start
        key_pull = jnp.concatenate(
            [
                jnp.where(strict, scores[head * ROWS : (head + 1) * ROWS, ROWS:], 0.0)
                for head in range(2)
            ],
            axis=1,
        ).astype(BF16)
        pulled = dot(key_pull, two_heads(value))
        wanted = jnp.concatenate([pulled, left_prev * from_start], axis=1).astype(BF16)
        solved = dot(jnp.concatenate(inverses, axis=1), two_heads(wanted)).astype(BF16)
        uw[pair] = solved
        tail_insert = (right_insert * to_end).astype(BF16)
        tail_key = (right_key * to_end).astype(BF16)
        both = t_dot(solved, tail_insert)
        ends = both[:PAIR] + t_dot(value, tail_key)
        moved = both[PAIR:]
        moved = moved + jnp.where(row == col, jnp.exp(final) - 1.0, 0.0)
        left_lanes = left_half((HEAD, PAIR))
        moved = jnp.where(left_lanes, moved[:HEAD], moved[HEAD:])
        ends = jnp.where(left_lanes, ends[:HEAD], ends[HEAD:])
        for head in range(2):
            moved_part = packed(moved, head).astype(BF16)
            for half in range(2):
                unit_at = pair * 4 + head * 2 + half
                msg[unit_at, 0:32] = moved_part
                msg[unit_at, 32:48] = packed(ends[half * 32 : half * 32 + 32], head).astype(BF16)


def local_terms(pair, aik, uw, vv, srd, local, start_map):
    solved = two_heads(uw[pair])
    scores = aik[pair]
    read = dot(scores[:, : 2 * ROWS], solved)
    keyed = dot(scores[:, 2 * ROWS :], two_heads(vv[pair]))
    local[pair] = read[:, :PAIR] + keyed
    start_map[pair] = (srd[pair] + read[:, PAIR:]).astype(BF16)


def scanned(n_seq, backward, recv, ret, inside):
    def place(i):
        return i + backward * (n_seq - 1 - 2 * i)

    size = 4
    groups = n_seq // size
    left = left_half((HEAD + 32, PAIR))
    blank = jnp.zeros((HEAD, PAIR), BF16)

    def block(i):
        value = recv[place(i)].astype(F32)
        whole = jnp.concatenate([unpacked(value[:32]), unpacked(value[32:])], axis=0)
        return jnp.where(left, whole, 0.0)

    def through(state, mapping):
        full = jnp.concatenate([mapping.astype(BF16), blank], axis=0)
        return dot(state.astype(BF16), full)

    for k in range(size):
        for g in range(groups):
            new = block(g * size + k)
            if k:
                so_far = inside[g * size + k - 1]
                new = so_far + new + through(so_far, new[:HEAD])
            inside[g * size + k] = new

    def onward(g, state):
        whole = inside[g * size + size - 1]
        for k in range(size):
            here = state
            if k:
                before = inside[g * size + k - 1]
                here = here + before[HEAD:] + through(here, before[:HEAD])
            ret[place(g * size + k)] = packed(here, 0).astype(BF16)
        return state + whole[HEAD:] + through(state, whole[:HEAD])

    lax.fori_loop(0, groups, onward, jnp.zeros((32, PAIR), F32))


def incoming(pair, states):
    rows = []
    left = left_half((16, PAIR))
    for head in range(2):
        for half in range(2):
            value = states[pair * 4 + head * 2 + half].astype(F32)
            turned = pltpu.roll(value, HEAD, 1)
            if head == 0:
                rows += [jnp.where(left, value, 0.0), jnp.where(left, turned, 0.0)]
            else:
                rows += [jnp.where(left, 0.0, turned), jnp.where(left, 0.0, value)]
    return jnp.concatenate(rows, axis=0).astype(BF16)


def grouped(pair, states, local, start_map, ones):
    out = local[pair] + dot_t(start_map[pair], incoming(pair, states))
    high, low = halves(out)
    centered = out - (dot(high, ones) + dot(low, ones)) * (1.0 / HEAD)
    spread = dot((centered * centered).astype(BF16), ones) * (1.0 / HEAD)
    return centered * lax.rsqrt(spread + GROUP_EPS)


def kernel(
    n_seq, n_mp,
    ids, hidden_fwd, hidden_rc, embed, gain1, gain2, mix,
    w_r, w_k, w_v, d_first, d_base, d_second, c_first, i_base, c_second,
    group_gain, w_out, ffn_key, ffn_value,
    out,
    wr, wk, wv, fk, fv, wo,
    xf, xr, rc_own, embf, prev, nxt, ids_prev, ids_next,
    st, nrm, mx, proj, masks, msg, recv, ret, states, aik, uw, vv, srd, local, start_map,
    joined, residual, act, part, got, inside,
    lsem, ss1, rs1, ss2, rs2, ss3, rs3, ss4, rs4,
):
    j, m = lax.axis_index("seq"), lax.axis_index("mp")

    def seq_at(offset):
        return lax.rem(j + offset + n_seq, n_seq)

    def mp_at(offset):
        return lax.rem(m + offset, n_mp)

    def send(src, dst, sems, index, device):
        copy = pltpu.make_async_remote_copy(
            src_ref=src, dst_ref=dst, send_sem=sems[0].at[index], recv_sem=sems[1].at[index],
            device_id=device, device_id_type=MESH,
        )
        copy.start()
        return copy

    def fetch(src, dst, index):
        copy = pltpu.make_async_copy(src, dst, lsem.at[index])
        copy.start()
        return copy

    barrier = pltpu.get_barrier_semaphore()

    def greet(seq_to, mp_to):
        pl.semaphore_signal(barrier, inc=1, device_id=(seq_to, mp_to), device_id_type=MESH)

    for k in range(1, n_mp):
        greet(j, mp_at(k))
        greet(seq_at(1), mp_at(k))
        greet(seq_at(-1), mp_at(k))

    def greet_far(d, carry):
        greet(seq_at(d), m)
        return carry

    lax.fori_loop(1, n_seq, greet_far, None)

    weights = [
        fetch(src, dst, i)
        for i, (src, dst) in enumerate(
            [(w_r, wr), (w_k, wk), (w_v, wv), (ffn_key, fk), (ffn_value, fv)]
        )
    ]
    own = [
        fetch(hidden_fwd, xf.at[m], 5),
        fetch(embed, embf.at[m], 6),
        fetch(w_out, wo.at[m], 7),
    ]
    masks_into(masks)
    pl.semaphore_wait(barrier, 3 * (n_mp - 1) + n_seq - 1)

    one = (ss1, rs1)
    copies = {}
    copies["mirror"] = send(hidden_rc, rc_own, one, 16, (n_seq - 1 - j, m))
    for k in range(1, n_mp):
        copies["emb", k] = send(embed, embf.at[m], one, 2 + k, (j, mp_at(k)))
        copies["fwd", k] = send(hidden_fwd, xf.at[m], one, k - 1, (j, mp_at(k)))
    for k in range(n_mp):
        copies["f_up", k] = send(
            hidden_fwd.at[pl.ds(ROWS - 16, 16)], prev.at[0, m], one, 6 + k, (seq_at(1), mp_at(k))
        )
        copies["f_down", k] = send(
            hidden_fwd.at[pl.ds(0, 16)], nxt.at[0, m], one, 10 + k, (seq_at(-1), mp_at(k))
        )
    copies["i_up"] = send(ids, ids_prev, one, 14, (seq_at(1), m))
    copies["i_down"] = send(ids, ids_next, one, 15, (seq_at(-1), m))

    letters = jnp.transpose(jnp.broadcast_to(ids[...].astype(F32), (ROWS, ROWS)))
    gain = gain1[...]
    has_prev = (j > 0).astype(F32)
    has_next = (j < n_seq - 1).astype(F32)

    def edges(b):
        sign, base = (1.0, 0.0) if b == 0 else (-1.0, 3.0)
        before = base + sign * ids_prev[0:1, ROWS - 1 : ROWS].astype(F32)
        after = base + sign * ids_next[0:1, 0:1].astype(F32)
        last, first = (15, 0) if b == 0 else (0, 15)
        nrm[7:8] = edge_row(prev.at[b], last, before, embf, gain, has_prev)
        nrm[136:137] = edge_row(nxt.at[b], first, after, embf, gain, has_next)

    def strand(b):
        normed_and_mixed(b, st, nrm, mx, gain, mix)
        projected(mx, wr, wk, wv, d_first, d_base, d_second, c_first, i_base, c_second, proj)

        def body(q, carry):
            block_terms(b, q, proj, masks, msg, aik, uw, vv, srd)
            return carry

        lax.fori_loop(0, 2, body, None)

    copies["mirror"].wait_recv()
    for k in range(1, n_mp):
        copies["rc", k] = send(rc_own, xr.at[m], one, 16 + k, (j, mp_at(k)))
    for k in range(n_mp):
        copies["r_up", k] = send(
            rc_own.at[pl.ds(0, 16)], prev.at[1, m], one, 20 + k, (seq_at(1), mp_at(k))
        )
        copies["r_down", k] = send(
            rc_own.at[pl.ds(ROWS - 16, 16)], nxt.at[1, m], one, 24 + k, (seq_at(-1), mp_at(k))
        )
    own_rc = fetch(rc_own, xr.at[m], 8)
    sibling = m + 1 - 2 * lax.rem(m, 2)
    across = mp_at(2)
    copies["w_near"] = send(w_out, wo.at[m], one, 28, (j, sibling))
    copies["w_far"] = send(w_out, wo.at[m], one, 29, (j, across))

    for copy in own:
        copy.wait()
    for k in range(1, n_mp):
        copies["emb", k].wait_recv()
        copies["fwd", k].wait_recv()
    for k in range(n_mp):
        copies["f_up", k].wait_recv()
        copies["f_down", k].wait_recv()
    copies["i_up"].wait_recv()
    copies["i_down"].wait_recv()
    strand_rows(
        0, lambda t: xf[t // 2, :, (t % 2) * PAIR : (t % 2 + 1) * PAIR].astype(F32),
        letters, embf, st,
    )
    edges(0)
    for copy in weights[:3]:
        copy.wait()
    strand(0)

    own_rc.wait()
    for k in range(1, n_mp):
        copies["rc", k].wait_recv()
    for k in range(n_mp):
        copies["r_up", k].wait_recv()
        copies["r_down", k].wait_recv()
    turn = jnp.where(
        iota2((ROWS, ROWS), 0) + iota2((ROWS, ROWS), 1) == ROWS - 1, 1.0, 0.0
    ).astype(BF16)
    strand_rows(
        1, lambda t: dot(turn, xr[t // 2, :, (t % 2) * PAIR : (t % 2 + 1) * PAIR]),
        3.0 - letters, embf, st,
    )
    edges(1)
    strand(1)

    def to_unit(d):
        return pltpu.make_async_remote_copy(
            src_ref=msg.at[seq_at(d)], dst_ref=recv.at[j],
            send_sem=ss2.at[d], recv_sem=rs2.at[d],
            device_id=(seq_at(d), m), device_id_type=MESH,
        )

    def to_block(d):
        return pltpu.make_async_remote_copy(
            src_ref=ret.at[seq_at(d)], dst_ref=states.at[j],
            send_sem=ss3.at[d], recv_sem=rs3.at[d],
            device_id=(seq_at(d), m), device_id_type=MESH,
        )

    def each(action):
        def body(d, carry):
            action(d)
            return carry

        lax.fori_loop(1, n_seq, body, None)

    each(lambda d: to_unit(d).start())
    own_msg = fetch(msg.at[j], recv.at[j], 9)
    copies["w_far"].wait_recv()
    copies["w_on"] = send(wo.at[across], wo.at[across], one, 30, (j, sibling))

    def local_body(pair, carry):
        local_terms(pair, aik, uw, vv, srd, local, start_map)
        return carry

    lax.fori_loop(0, 8, local_body, None)
    own_msg.wait()
    each(lambda d: to_unit(d).wait_recv())
    scanned(n_seq, j // (n_seq // 2), recv, ret, inside)
    each(lambda d: to_block(d).start())
    own_ret = fetch(ret.at[j], states.at[j], 10)
    own_ret.wait()
    each(lambda d: to_block(d).wait_recv())

    same_head = iota2((PAIR, PAIR), 0) // HEAD == iota2((PAIR, PAIR), 1) // HEAD
    ones = jnp.where(same_head, 1.0, 0.0).astype(BF16)
    four = (ss4, rs4)
    for b in range(2):
        for q in range(2):
            total = grouped(b * 2 + q, states, local, start_map, ones) + grouped(
                4 + b * 2 + q, states, local, start_map, ones
            )
            lanes = slice(q * PAIR, (q + 1) * PAIR)
            joined[m, b * ROWS : (b + 1) * ROWS, lanes] = (
                total * group_gain[:, lanes]
            ).astype(BF16)
        for k in range(1, n_mp):
            block = joined.at[m, pl.ds(b * ROWS, ROWS)]
            copies["join", b, k] = send(block, block, four, b * 3 + k - 1, (j, mp_at(k)))

    copies["w_near"].wait_recv()
    copies["w_on"].wait_recv()
    for copy in weights[3:]:
        copy.wait()
    for b in range(2):
        for k in range(1, n_mp):
            copies["join", b, k].wait_recv()
        rows = slice(b * ROWS, (b + 1) * ROWS)
        whole = st[b].astype(F32)
        for s in range(n_mp):
            whole = whole + dot(joined[s, rows], wo[s])
        residual[rows] = whole
        ffn_in = layer_norm(whole, gain2[...]).astype(BF16)
        act[rows] = jnp.square(jnp.maximum(dot(ffn_in, fk[...]), 0.0)).astype(BF16)

    def partial(index):
        lanes = pl.ds(pl.multiple_of(index * 2 * PAIR, PAIR), 2 * PAIR)
        both = dot(act[...], fv[:, lanes])
        return both[:ROWS] + both[ROWS:], lanes

    for k in range(1, n_mp):
        peer = mp_at(k)
        value, _ = partial(peer)
        part[k - 1] = value.astype(BF16)
        copies["sum", k] = send(part.at[k - 1], got.at[k - 1], four, 5 + k, (j, peer))
    value, lanes = partial(m)
    value = value + residual[:ROWS, lanes] + residual[ROWS:, lanes]
    for k in range(1, n_mp):
        copies["sum", k].wait_recv()
        value = value + got[k - 1].astype(F32)
    out[...] = value.astype(BF16)

    for copy in copies.values():
        copy.wait_send()
    each(lambda d: to_unit(d).wait_send())
    each(lambda d: to_block(d).wait_send())


def on_device(n_seq, n_mp, *args):
    args = list(args)
    args[0] = args[0].reshape(1, ROWS)
    for index in (4, 5, 11, 14, 16):
        args[index] = args[index].reshape(1, -1)
    in_place = {1, 2, 7, 8, 9, 17, 18, 19}
    vmem = pltpu.VMEM
    dma = pltpu.SemaphoreType.DMA
    width = 2 * PAIR
    scratch = [
        vmem((1024, width), BF16), vmem((1024, width), BF16), vmem((1024, width), BF16),
        vmem((1024, 1024), BF16), vmem((1024, 1024), BF16), vmem((n_mp, width, 1024), BF16),
        vmem((n_mp, ROWS, width), BF16), vmem((n_mp, ROWS, width), BF16),
        vmem((ROWS, width), BF16), vmem((n_mp, 4, width), F32),
        vmem((2, n_mp, 16, width), BF16), vmem((2, n_mp, 16, width), BF16),
        vmem((1, ROWS), jnp.int32), vmem((1, ROWS), jnp.int32),
        vmem((2, ROWS, 1024), BF16), vmem((144, 1024), F32), vmem((5, 2 * ROWS, 1024), BF16),
        vmem((7, 2, 2, ROWS, PAIR), F32), vmem((2, LEVELS, ROWS, ROWS), BF16),
        vmem((32, 48, PAIR), BF16), vmem((n_seq, 48, PAIR), BF16),
        vmem((n_seq, 16, PAIR), BF16), vmem((32, 16, PAIR), BF16),
        vmem((8, ROWS, 4 * ROWS), BF16), vmem((8, ROWS, width), BF16),
        vmem((8, ROWS, PAIR), BF16), vmem((8, ROWS, PAIR), F32),
        vmem((8, ROWS, PAIR), F32), vmem((8, ROWS, PAIR), BF16),
        vmem((n_mp, 2 * ROWS, width), BF16), vmem((2 * ROWS, 1024), F32),
        vmem((2 * ROWS, 1024), BF16), vmem((3, ROWS, width), BF16), vmem((3, ROWS, width), BF16),
        vmem((n_seq, 96, PAIR), F32),
        dma((11,)), dma((32,)), dma((32,)), dma((n_seq,)), dma((n_seq,)),
        dma((n_seq,)), dma((n_seq,)), dma((9,)), dma((9,)),
    ]
    return pl.pallas_call(
        functools.partial(kernel, n_seq, n_mp),
        out_shape=jax.ShapeDtypeStruct((ROWS, width), BF16),
        in_specs=[
            pl.BlockSpec(memory_space=pl.ANY if i in in_place else pltpu.VMEM)
            for i in range(len(args))
        ],
        out_specs=pl.BlockSpec(memory_space=pltpu.VMEM),
        scratch_shapes=scratch,
        compiler_params=pltpu.CompilerParams(
            collective_id=0, has_side_effects=True, vmem_limit_bytes=60 * 1024 * 1024
        ),
    )(*args)


def solution(mesh):
    seq, split, rows = P("seq", "mp"), P(None, "mp"), P("mp", None)
    vec, all_ = P("mp"), P()
    placed = (
        P("seq"), seq, seq, split, all_, all_, all_, split, split, split,
        all_, vec, split, all_, vec, split, vec, rows, split, rows,
    )
    return jax.shard_map(
        functools.partial(on_device, mesh.shape["seq"], mesh.shape["mp"]),
        mesh=mesh, in_specs=placed, out_specs=seq, check_vma=False,
    )
```

time: 425 us -> 86.5 us (0.20)
  the two profiles are of different devices: /device:TPU:0 before, /device:TPU:1 now
where the time goes in v1:
time: 86.5 us; the launch traced here: 86.3 us
  Pallas kernels  81.4 us (94%)
  local copies, waits for them, and re-layouts  4.95 us (6%)
    pallas_call x1, Pallas kernels, on_device(): pl.pallas_call(functools.partial(kernel, n_seq, n_mp), out_shape=jax.Shap...  81.4 us
    unnamed x3, local copies, waits for them, and re-layouts  4.95 us

profile of v1, /device:TPU:1, one launch (start us, length us, event | category | flops | bytes accessed | tf_op | source)
XLA Modules:
  0.0 86.3 jit_solution(16181692435988484525)
XLA Ops:
  0.0 1.7 %copy.21.d_first = bf16[1024,64]{1,0:T(8,128)(2,1)} copy(bf16[1024,64]{0,1:T(8,128)(2,1)} %param.30) | data formatting | bytes 262144 | tf_op args[10]
  1.7 1.7 %copy.22.c_first = bf16[1024,64]{1,0:T(8,128)(2,1)} copy(bf16[1024,64]{0,1:T(8,128)(2,1)} %param.33) | data formatting | bytes 262144 | tf_op args[13]
  3.5 81.4 %shard_map.190 = bf16[128,256]{1,0:T(8,128)(2,1)} custom-call(s32[1,128]{1,0:T(1,128)} %bitcast.11, bf16[128,256]{1,0:T(8,128)(2,1)} %hidden_fwd.1, bf16[128,256]{1,0:T(8,128)(2,1)} %hidden_rc.1, f32[4,256]{1,0:T(4,128)} %embed.1, f32[1,1024]{1,0:T(1,128)} %bitcast.6, f32[1,1024]{1,0:T(1,128)} %bitcast.7, f32[5,1024]{1,0:T(8,128)} %mix.1, ...), custom_call_target="tpu_custom_call" | custom-call | tf_op jit(solution)/shard_map/pallas_call | solution.py:568
  84.8 1.5 %copy.24 = bf16[128,256]{1,0:T(8,128)(2,1)} copy(bf16[128,256]{1,0:T(8,128)(2,1)} %shard_map.190) | data formatting | bytes 131072

commit v2 on v1

--- a/solution.py
+++ b/solution.py
@@ -132,9 +132,9 @@
     high, low = halves(key * key)
     square = dot(high, ones) + dot(low, ones)
     keep(3, key * lax.rsqrt(square + UNIT_EPS))
-    low_iclr = dot(mx[4], cfw[...]).astype(BF16)
+    low_iclr = dot_t(mx[4], cfw[...]).astype(BF16)
     keep(4, jax.nn.sigmoid(ibase[...] + dot(low_iclr, csw[...])))
-    low_decay = jnp.tanh(dot(mx[3], dfw[...])).astype(BF16)
+    low_decay = jnp.tanh(dot_t(mx[3], dfw[...])).astype(BF16)
     log_decay = -DECAY_SCALE * jax.nn.sigmoid(dbase[...] + dot(low_decay, dsw[...]))
     keep(5, log_decay)
     row, col = iota2((ROWS, ROWS), 0), iota2((ROWS, ROWS), 1)
@@ -147,69 +147,68 @@
     keep(6, jnp.concatenate(totals, axis=0))
 
 
-def block_terms(b, q, proj, masks, msg, aik, uw, vv, srd):
+def block_terms(b, proj, masks, msg, aik, uw, vv, srd):
     row, col = iota2((ROWS, ROWS), 0), iota2((ROWS, ROWS), 1)
-    eye = jnp.where(row == col, 1.0, 0.0)
+    eye = jnp.where(row == col, 1.0, 0.0).astype(BF16)
+    chains, later = [], []
     for beta in range(2):
-        pair = (beta * 2 + b) * 2 + q
-        receptance, key, value, unit, iclr, log_decay, total = [
-            proj[i, beta, q] for i in range(7)
-        ]
-        middle = total[64:65] if beta == 0 else total[63:64]
-        final = total[127:128] if beta == 0 else total[0:1]
-        scale_here = jnp.exp(total - middle)
-        scale_right = jnp.exp(middle - total)
-        left_prev = -unit * jnp.exp(total - log_decay - middle)
-        left_here = receptance * scale_here
-        right_insert = iclr * unit * scale_right
-        right_key = key * scale_right
-        from_start = jnp.exp(middle)
-        to_end = jnp.exp(final - middle)
-        left = jnp.concatenate(
-            [two_heads(left_prev.astype(BF16)), two_heads(left_here.astype(BF16))], axis=0
-        )
-        right = jnp.concatenate([right_insert, right_key], axis=0).astype(BF16)
-        scores = dot_t(left, right)
         strict = (row > col) if beta == 0 else (row < col)
         inclusive = (row >= col) if beta == 0 else (row <= col)
-        inverses = []
-        for head in range(2):
-            lower = jnp.where(strict, scores[head * ROWS : (head + 1) * ROWS, :ROWS], 0.0)
-            lower = lower.astype(BF16)
-            inverse = eye + (lower * masks[beta, 0]).astype(F32)
-            for level in range(1, LEVELS):
-                narrow = inverse.astype(BF16)
-                step = dot(narrow, lower * masks[beta, level]).astype(BF16)
-                inverse = inverse + dot(step, narrow)
-            inverses.append(inverse.astype(BF16))
-            at = 2 * ROWS + head * ROWS
-            aik[pair, :, head * ROWS : (head + 1) * ROWS] = jnp.where(
-                inclusive, scores[at : at + ROWS, :ROWS], 0.0
-            ).astype(BF16)
-            aik[pair, :, (2 + head) * ROWS : (3 + head) * ROWS] = jnp.where(
-                inclusive, scores[at : at + ROWS, ROWS:], 0.0
-            ).astype(BF16)
-        value = value.astype(BF16)
-        vv[pair] = value
-        srd[pair] = left_here * from_start
-        key_pull = jnp.concatenate(
-            [
-                jnp.where(strict, scores[head * ROWS : (head + 1) * ROWS, ROWS:], 0.0)
-                for head in range(2)
-            ],
-            axis=1,
-        ).astype(BF16)
-        pulled = dot(key_pull, two_heads(value))
-        wanted = jnp.concatenate([pulled, left_prev * from_start], axis=1).astype(BF16)
-        solved = dot(jnp.concatenate(inverses, axis=1), two_heads(wanted)).astype(BF16)
+        for q in range(2):
+            pair = (beta * 2 + b) * 2 + q
+            receptance, key, value, unit, iclr, log_decay, total = [
+                proj[i, beta, q] for i in range(7)
+            ]
+            middle = total[64:65] if beta == 0 else total[63:64]
+            final = total[127:128] if beta == 0 else total[0:1]
+            scale_right = jnp.exp(middle - total)
+            left_prev = -unit * jnp.exp(total - log_decay - middle)
+            left_here = receptance * jnp.exp(total - middle)
+            right_insert = iclr * unit * scale_right
+            right_key = key * scale_right
+            from_start = jnp.exp(middle)
+            to_end = jnp.exp(final - middle)
+            left = jnp.concatenate(
+                [two_heads(left_prev.astype(BF16)), two_heads(left_here.astype(BF16))], axis=0
+            )
+            right = jnp.concatenate([right_insert, right_key], axis=0).astype(BF16)
+            scores = dot_t(left, right)
+            pulls = []
+            for head in range(2):
+                at = head * ROWS
+                lower = jnp.where(strict, scores[at : at + ROWS, :ROWS], 0.0).astype(BF16)
+                chains.append([beta, lower, eye + lower * masks[beta, 0]])
+                pulls.append(jnp.where(strict, scores[at : at + ROWS, ROWS:], 0.0).astype(BF16))
+                read = 2 * ROWS + at
+                aik[pair, :, at : at + ROWS] = jnp.where(
+                    inclusive, scores[read : read + ROWS, :ROWS], 0.0
+                ).astype(BF16)
+                aik[pair, :, 2 * ROWS + at : 3 * ROWS + at] = jnp.where(
+                    inclusive, scores[read : read + ROWS, ROWS:], 0.0
+                ).astype(BF16)
+            value = value.astype(BF16)
+            vv[pair] = value
+            srd[pair] = left_here * from_start
+            pulled = dot(jnp.concatenate(pulls, axis=1), two_heads(value))
+            wanted = jnp.concatenate([pulled, left_prev * from_start], axis=1).astype(BF16)
+            tail_insert = (right_insert * to_end).astype(BF16)
+            tail_key = (right_key * to_end).astype(BF16)
+            later.append((pair, wanted, value, tail_insert, tail_key, final))
+    for level in range(1, LEVELS):
+        steps = [
+            dot(inverse, lower * masks[beta, level]).astype(BF16)
+            for beta, lower, inverse in chains
+        ]
+        for chain, step in zip(chains, steps):
+            chain[2] = chain[2] + dot(step, chain[2]).astype(BF16)
+    left_lanes = left_half((HEAD, PAIR))
+    for index, (pair, wanted, value, tail_insert, tail_key, final) in enumerate(later):
+        inverses = jnp.concatenate([chains[2 * index][2], chains[2 * index + 1][2]], axis=1)
+        solved = dot(inverses, two_heads(wanted)).astype(BF16)
         uw[pair] = solved
-        tail_insert = (right_insert * to_end).astype(BF16)
-        tail_key = (right_key * to_end).astype(BF16)
         both = t_dot(solved, tail_insert)
         ends = both[:PAIR] + t_dot(value, tail_key)
-        moved = both[PAIR:]
-        moved = moved + jnp.where(row == col, jnp.exp(final) - 1.0, 0.0)
-        left_lanes = left_half((HEAD, PAIR))
+        moved = both[PAIR:] + jnp.where(row == col, jnp.exp(final) - 1.0, 0.0)
         moved = jnp.where(left_lanes, moved[:HEAD], moved[HEAD:])
         ends = jnp.where(left_lanes, ends[:HEAD], ends[HEAD:])
         for head in range(2):
@@ -229,7 +228,7 @@
     start_map[pair] = (srd[pair] + read[:, PAIR:]).astype(BF16)
 
 
-def scanned(n_seq, backward, recv, ret, inside):
+def scanned(n_seq, backward, recv, ret, inside, give):
     def place(i):
         return i + backward * (n_seq - 1 - 2 * i)
 
@@ -263,6 +262,7 @@
                 before = inside[g * size + k - 1]
                 here = here + before[HEAD:] + through(here, before[:HEAD])
             ret[place(g * size + k)] = packed(here, 0).astype(BF16)
+
         return state + whole[HEAD:] + through(state, whole[:HEAD])
 
     lax.fori_loop(0, groups, onward, jnp.zeros((32, PAIR), F32))
@@ -385,12 +385,41 @@
     def strand(b):
         normed_and_mixed(b, st, nrm, mx, gain, mix)
         projected(mx, wr, wk, wv, d_first, d_base, d_second, c_first, i_base, c_second, proj)
-
-        def body(q, carry):
-            block_terms(b, q, proj, masks, msg, aik, uw, vv, srd)
+        block_terms(b, proj, masks, msg, aik, uw, vv, srd)
+
+    def to_unit(d):
+        return pltpu.make_async_remote_copy(
+            src_ref=msg.at[seq_at(d)], dst_ref=recv.at[j],
+            send_sem=ss2.at[d], recv_sem=rs2.at[d],
+            device_id=(seq_at(d), m), device_id_type=MESH,
+        )
+
+    def give(block):
+        @pl.when(block != j)
+        def _():
+            to_block(lax.rem(block - j + n_seq, n_seq)).start()
+
+    def to_block(d):
+        return pltpu.make_async_remote_copy(
+            src_ref=ret.at[seq_at(d)], dst_ref=states.at[j],
+            send_sem=ss3.at[d], recv_sem=rs3.at[d],
+            device_id=(seq_at(d), m), device_id_type=MESH,
+        )
+
+    def each(action):
+        def body(d, carry):
+            action(d)
             return carry
 
-        lax.fori_loop(0, 2, body, None)
+        lax.fori_loop(1, n_seq, body, None)
+
+    def give_units(b):
+        def start(d):
+            @pl.when(lax.rem(seq_at(d) // 8, 2) == b)
+            def _():
+                to_unit(d).start()
+
+        each(start)
 
     copies["mirror"].wait_recv()
     for k in range(1, n_mp):
@@ -426,6 +455,7 @@
     for copy in weights[:3]:
         copy.wait()
     strand(0)
+    give_units(0)
 
     own_rc.wait()
     for k in range(1, n_mp):
@@ -443,28 +473,7 @@
     edges(1)
     strand(1)
 
-    def to_unit(d):
-        return pltpu.make_async_remote_copy(
-            src_ref=msg.at[seq_at(d)], dst_ref=recv.at[j],
-            send_sem=ss2.at[d], recv_sem=rs2.at[d],
-            device_id=(seq_at(d), m), device_id_type=MESH,
-        )
-
-    def to_block(d):
-        return pltpu.make_async_remote_copy(
-            src_ref=ret.at[seq_at(d)], dst_ref=states.at[j],
-            send_sem=ss3.at[d], recv_sem=rs3.at[d],
-            device_id=(seq_at(d), m), device_id_type=MESH,
-        )
-
-    def each(action):
-        def body(d, carry):
-            action(d)
-            return carry
-
-        lax.fori_loop(1, n_seq, body, None)
-
-    each(lambda d: to_unit(d).start())
+    give_units(1)
     own_msg = fetch(msg.at[j], recv.at[j], 9)
     copies["w_far"].wait_recv()
     copies["w_on"] = send(wo.at[across], wo.at[across], one, 30, (j, sibling))
@@ -476,7 +485,7 @@
     lax.fori_loop(0, 8, local_body, None)
     own_msg.wait()
     each(lambda d: to_unit(d).wait_recv())
-    scanned(n_seq, j // (n_seq // 2), recv, ret, inside)
+    scanned(n_seq, j // (n_seq // 2), recv, ret, inside, give)
     each(lambda d: to_block(d).start())
     own_ret = fetch(ret.at[j], states.at[j], 10)
     own_ret.wait()
@@ -494,17 +503,21 @@
             joined[m, b * ROWS : (b + 1) * ROWS, lanes] = (
                 total * group_gain[:, lanes]
             ).astype(BF16)
-        for k in range(1, n_mp):
-            block = joined.at[m, pl.ds(b * ROWS, ROWS)]
-            copies["join", b, k] = send(block, block, four, b * 3 + k - 1, (j, mp_at(k)))
+        block = joined.at[m, pl.ds(b * ROWS, ROWS)]
+        copies["join", b, 1] = send(block, block, four, b * 3 + 1, (j, across))
+        copies["join", b, 0] = send(block, block, four, b * 3, (j, sibling))
+    for b in range(2):
+        block = joined.at[across, pl.ds(b * ROWS, ROWS)]
+        copies["join", b, 1].wait_recv()
+        copies["join", b, 2] = send(block, block, four, b * 3 + 2, (j, sibling))
 
     copies["w_near"].wait_recv()
     copies["w_on"].wait_recv()
     for copy in weights[3:]:
         copy.wait()
     for b in range(2):
-        for k in range(1, n_mp):
-            copies["join", b, k].wait_recv()
+        copies["join", b, 0].wait_recv()
+        copies["join", b, 2].wait_recv()
         rows = slice(b * ROWS, (b + 1) * ROWS)
         whole = st[b].astype(F32)
         for s in range(n_mp):
@@ -541,6 +554,8 @@
     args[0] = args[0].reshape(1, ROWS)
     for index in (4, 5, 11, 14, 16):
         args[index] = args[index].reshape(1, -1)
+    for index in (10, 13):
+        args[index] = args[index].T
     in_place = {1, 2, 7, 8, 9, 17, 18, 19}
     vmem = pltpu.VMEM
     dma = pltpu.SemaphoreType.DMA

time: 86.5 us -> 65.5 us (0.76)
  Pallas kernels: 81.4 us -> 63.9 us
  local copies, waits for them, and re-layouts: 4.95 us -> 1.47 us
    pallas_call x1, Pallas kernels: 81.4 us -> 63.9 us  [on_device(): pl.pallas_call(functools.partial(kernel, n_seq, n_mp), out_shape=jax.Shap...]
    unnamed x3 -> x1, local copies, waits for them, and re-layouts: 4.95 us -> 1.47 us
where the time goes in v2:
time: 65.5 us; the launch traced here: 65.3 us
  Pallas kernels  63.9 us (98%)
  local copies, waits for them, and re-layouts  1.47 us (2%)
    pallas_call x1, Pallas kernels, on_device(): pl.pallas_call(functools.partial(kernel, n_seq, n_mp), out_shape=jax.Shap...  63.9 us
    unnamed x1, local copies, waits for them, and re-layouts  1.47 us

profile of v2, /device:TPU:1, one launch (start us, length us, event | category | flops | bytes accessed | tf_op | source)
XLA Modules:
  0.0 65.3 jit_solution(6851371695278820078)
XLA Ops:
  0.0 63.9 %shard_map.190 = bf16[128,256]{1,0:T(8,128)(2,1)} custom-call(s32[1,128]{1,0:T(1,128)} %bitcast.15, bf16[128,256]{1,0:T(8,128)(2,1)} %hidden_fwd.1, bf16[128,256]{1,0:T(8,128)(2,1)} %hidden_rc.1, f32[4,256]{1,0:T(4,128)} %embed.1, f32[1,1024]{1,0:T(1,128)} %bitcast.10, f32[1,1024]{1,0:T(1,128)} %bitcast.11, f32[5,1024]{1,0:T(8,128)} %mix.1, ...), custom_call_target="tpu_custom_call" | custom-call | tf_op jit(solution)/shard_map/pallas_call | solution.py:583
  63.9 1.5 %copy.22 = bf16[128,256]{1,0:T(8,128)(2,1)} copy(bf16[128,256]{1,0:T(8,128)(2,1)} %shard_map.190) | data formatting | bytes 131072

commit v3 on v2

--- a/solution.py
+++ b/solution.py
@@ -64,6 +64,12 @@
     left = left_half(value.shape)
     zero = jnp.zeros_like(value)
     return jnp.concatenate([jnp.where(left, value, zero), jnp.where(left, zero, value)], axis=0)
+
+
+def on_diagonal(first, second):
+    zero = jnp.zeros_like(first)
+    upper = jnp.concatenate([first, zero], axis=1)
+    return jnp.concatenate([upper, jnp.concatenate([zero, second], axis=1)], axis=0)
 
 
 def packed(value, head):
@@ -173,11 +179,11 @@
             )
             right = jnp.concatenate([right_insert, right_key], axis=0).astype(BF16)
             scores = dot_t(left, right)
-            pulls = []
+            pulls, lowers = [], []
             for head in range(2):
                 at = head * ROWS
                 lower = jnp.where(strict, scores[at : at + ROWS, :ROWS], 0.0).astype(BF16)
-                chains.append([beta, lower, eye + lower * masks[beta, 0]])
+                lowers.append(lower)
                 pulls.append(jnp.where(strict, scores[at : at + ROWS, ROWS:], 0.0).astype(BF16))
                 read = 2 * ROWS + at
                 aik[pair, :, at : at + ROWS] = jnp.where(
@@ -186,6 +192,8 @@
                 aik[pair, :, 2 * ROWS + at : 3 * ROWS + at] = jnp.where(
                     inclusive, scores[read : read + ROWS, ROWS:], 0.0
                 ).astype(BF16)
+            inverse = jnp.concatenate([eye + lower * masks[beta, 0] for lower in lowers], axis=1)
+            chains.append([beta, lowers, inverse])
             value = value.astype(BF16)
             vv[pair] = value
             srd[pair] = left_here * from_start
@@ -195,16 +203,29 @@
             tail_key = (right_key * to_end).astype(BF16)
             later.append((pair, wanted, value, tail_insert, tail_key, final))
     for level in range(1, LEVELS):
-        steps = [
-            dot(inverse, lower * masks[beta, level]).astype(BF16)
-            for beta, lower, inverse in chains
-        ]
+        size = 1 << level
+        steps = []
+        for beta, lowers, inverse in chains:
+            if size >= 16:
+                starts = range(0 if beta else size, ROWS, 2 * size)
+                inverse = jnp.concatenate([inverse[at : at + size] for at in starts], axis=0)
+            level_mask = masks[beta, level]
+            below = on_diagonal(*[lower * level_mask for lower in lowers])
+            steps.append(dot(inverse, below).astype(BF16))
         for chain, step in zip(chains, steps):
-            chain[2] = chain[2] + dot(step, chain[2]).astype(BF16)
+            beta, _, inverse = chain
+            step = dot(step, on_diagonal(inverse[:, :ROWS], inverse[:, ROWS:])).astype(BF16)
+            if size >= 16:
+                blocks = [inverse[at : at + size] for at in range(0, ROWS, size)]
+                for index in range(ROWS // (2 * size)):
+                    changed = 2 * index + 1 - beta
+                    blocks[changed] = blocks[changed] + step[index * size : (index + 1) * size]
+                chain[2] = jnp.concatenate(blocks, axis=0)
+            else:
+                chain[2] = inverse + step
     left_lanes = left_half((HEAD, PAIR))
     for index, (pair, wanted, value, tail_insert, tail_key, final) in enumerate(later):
-        inverses = jnp.concatenate([chains[2 * index][2], chains[2 * index + 1][2]], axis=1)
-        solved = dot(inverses, two_heads(wanted)).astype(BF16)
+        solved = dot(chains[index][2], two_heads(wanted)).astype(BF16)
         uw[pair] = solved
         both = t_dot(solved, tail_insert)
         ends = both[:PAIR] + t_dot(value, tail_key)
@@ -292,12 +313,13 @@
 
 def kernel(
     n_seq, n_mp,
-    ids, hidden_fwd, hidden_rc, embed, gain1, gain2, mix,
-    w_r, w_k, w_v, d_first, d_base, d_second, c_first, i_base, c_second,
-    group_gain, w_out, ffn_key, ffn_value,
+    ids_in, hidden_fwd, hidden_rc, embed, gain1_in, gain2_in, mix_in,
+    w_r, w_k, w_v, d_first_in, d_base_in, d_second_in, c_first_in, i_base_in, c_second_in,
+    group_gain_in, w_out, ffn_key, ffn_value,
     out,
+    ids, gain1, gain2, mix, d_first, d_base, d_second, c_first, i_base, c_second, group_gain,
     wr, wk, wv, fk, fv, wo,
-    xf, xr, rc_own, embf, prev, nxt, ids_prev, ids_next,
+    xf, xr, embf, prev, nxt, ids_prev, ids_next,
     st, nrm, mx, proj, masks, msg, recv, ret, states, aik, uw, vv, srd, local, start_map,
     joined, residual, act, part, got, inside,
     lsem, ss1, rs1, ss2, rs2, ss3, rs3, ss4, rs4,
@@ -318,6 +340,29 @@
         copy.start()
         return copy
 
+    def edge_act(act_remote, act_local):
+        for up in (True, False):
+            rows, place, seq_to = (0, prev, above) if up else (ROWS - 16, nxt, below)
+            source, target = hidden_rc.at[pl.ds(rows, 16)], place.at[1, m]
+
+            def remote(k, index=20 if up else 24, source=source, target=target, seq_to=seq_to):
+                act_remote(
+                    pltpu.make_async_remote_copy(
+                        src_ref=source, dst_ref=target,
+                        send_sem=ss1.at[index + k], recv_sem=rs1.at[index + k],
+                        device_id=(seq_to, mp_at(k)), device_id_type=MESH,
+                    )
+                )
+
+            pl.when(seq_to != j)(functools.partial(remote, 0))
+            for k in range(1, n_mp):
+                remote(k)
+            if act_local is not None:
+
+                @pl.when(seq_to == j)
+                def _(source=source, target=target, sem=lsem.at[21 + int(up)]):
+                    act_local(pltpu.make_async_copy(source, target, sem))
+
     def fetch(src, dst, index):
         copy = pltpu.make_async_copy(src, dst, lsem.at[index])
         copy.start()
@@ -325,6 +370,8 @@
 
     barrier = pltpu.get_barrier_semaphore()
 
+    above, below = lax.rem(n_seq - j, n_seq), lax.rem(2 * n_seq - 2 - j, n_seq)
+
     def greet(seq_to, mp_to):
         pl.semaphore_signal(barrier, inc=1, device_id=(seq_to, mp_to), device_id_type=MESH)
 
@@ -332,12 +379,16 @@
         greet(j, mp_at(k))
         greet(seq_at(1), mp_at(k))
         greet(seq_at(-1), mp_at(k))
+        greet(above, mp_at(k))
+        greet(below, mp_at(k))
 
     def greet_far(d, carry):
         greet(seq_at(d), m)
         return carry
 
     lax.fori_loop(1, n_seq, greet_far, None)
+    greet(n_seq - 1 - j, mp_at(2))
+    greet(j + 4 - 8 * lax.rem(j // 4, 2), mp_at(2))
 
     weights = [
         fetch(src, dst, i)
@@ -346,19 +397,28 @@
         )
     ]
     own = [
-        fetch(hidden_fwd, xf.at[m], 5),
-        fetch(embed, embf.at[m], 6),
-        fetch(w_out, wo.at[m], 7),
+        fetch(src, dst, 5 + i)
+        for i, (src, dst) in enumerate(
+            [
+                (hidden_fwd, xf.at[m]), (embed, embf.at[m]), (ids_in, ids), (gain1_in, gain1),
+                (mix_in, mix), (d_first_in, d_first), (d_base_in, d_base),
+                (d_second_in, d_second), (c_first_in, c_first), (i_base_in, i_base),
+                (c_second_in, c_second), (gain2_in, gain2), (group_gain_in, group_gain),
+                (w_out, wo.at[m]),
+            ]
+        )
     ]
     masks_into(masks)
-    pl.semaphore_wait(barrier, 3 * (n_mp - 1) + n_seq - 1)
+    pl.semaphore_wait(barrier, 5 * (n_mp - 1) + n_seq + 1)
 
     one = (ss1, rs1)
     copies = {}
-    copies["mirror"] = send(hidden_rc, rc_own, one, 16, (n_seq - 1 - j, m))
-    for k in range(1, n_mp):
-        copies["emb", k] = send(embed, embf.at[m], one, 2 + k, (j, mp_at(k)))
-        copies["fwd", k] = send(hidden_fwd, xf.at[m], one, k - 1, (j, mp_at(k)))
+    sibling = m + 1 - 2 * lax.rem(m, 2)
+    across = mp_at(2)
+    mirrored = n_seq - 1 - j
+    flipped = j + 4 - 8 * lax.rem(j // 4, 2)
+    copies["fwd", 1] = send(hidden_fwd, xf.at[m], one, 1, (j, across))
+    copies["fwd", 0] = send(hidden_fwd, xf.at[m], one, 0, (j, sibling))
     for k in range(n_mp):
         copies["f_up", k] = send(
             hidden_fwd.at[pl.ds(ROWS - 16, 16)], prev.at[0, m], one, 6 + k, (seq_at(1), mp_at(k))
@@ -366,11 +426,14 @@
         copies["f_down", k] = send(
             hidden_fwd.at[pl.ds(0, 16)], nxt.at[0, m], one, 10 + k, (seq_at(-1), mp_at(k))
         )
-    copies["i_up"] = send(ids, ids_prev, one, 14, (seq_at(1), m))
-    copies["i_down"] = send(ids, ids_next, one, 15, (seq_at(-1), m))
-
-    letters = jnp.transpose(jnp.broadcast_to(ids[...].astype(F32), (ROWS, ROWS)))
-    gain = gain1[...]
+    copies["i_up"] = send(ids_in, ids_prev, one, 14, (seq_at(1), m))
+    copies["i_down"] = send(ids_in, ids_next, one, 15, (seq_at(-1), m))
+    for k in range(1, n_mp):
+        copies["emb", k] = send(embed, embf.at[m], one, 2 + k, (j, mp_at(k)))
+    edge_act(lambda copy: copy.start(), lambda copy: copy.start())
+    copies["rc", 0] = send(hidden_rc, xr.at[m], one, 16, (mirrored, m))
+    copies["rc", 1] = send(hidden_rc, xr.at[m], one, 17, (mirrored, across))
+
     has_prev = (j > 0).astype(F32)
     has_next = (j < n_seq - 1).astype(F32)
 
@@ -379,11 +442,11 @@
         before = base + sign * ids_prev[0:1, ROWS - 1 : ROWS].astype(F32)
         after = base + sign * ids_next[0:1, 0:1].astype(F32)
         last, first = (15, 0) if b == 0 else (0, 15)
+        gain = gain1[...]
         nrm[7:8] = edge_row(prev.at[b], last, before, embf, gain, has_prev)
         nrm[136:137] = edge_row(nxt.at[b], first, after, embf, gain, has_next)
 
     def strand(b):
-        normed_and_mixed(b, st, nrm, mx, gain, mix)
         projected(mx, wr, wk, wv, d_first, d_base, d_second, c_first, i_base, c_second, proj)
         block_terms(b, proj, masks, msg, aik, uw, vv, srd)
 
@@ -421,27 +484,15 @@
 
         each(start)
 
-    copies["mirror"].wait_recv()
-    for k in range(1, n_mp):
-        copies["rc", k] = send(rc_own, xr.at[m], one, 16 + k, (j, mp_at(k)))
-    for k in range(n_mp):
-        copies["r_up", k] = send(
-            rc_own.at[pl.ds(0, 16)], prev.at[1, m], one, 20 + k, (seq_at(1), mp_at(k))
-        )
-        copies["r_down", k] = send(
-            rc_own.at[pl.ds(ROWS - 16, 16)], nxt.at[1, m], one, 24 + k, (seq_at(-1), mp_at(k))
-        )
-    own_rc = fetch(rc_own, xr.at[m], 8)
-    sibling = m + 1 - 2 * lax.rem(m, 2)
-    across = mp_at(2)
-    copies["w_near"] = send(w_out, wo.at[m], one, 28, (j, sibling))
-    copies["w_far"] = send(w_out, wo.at[m], one, 29, (j, across))
-
+    copies["fwd", 1].wait_recv()
+    copies["fwd", 2] = send(xf.at[across], xf.at[across], one, 2, (j, sibling))
     for copy in own:
         copy.wait()
+    letters = jnp.transpose(jnp.broadcast_to(ids[...].astype(F32), (ROWS, ROWS)))
     for k in range(1, n_mp):
         copies["emb", k].wait_recv()
-        copies["fwd", k].wait_recv()
+    copies["fwd", 0].wait_recv()
+    copies["fwd", 2].wait_recv()
     for k in range(n_mp):
         copies["f_up", k].wait_recv()
         copies["f_down", k].wait_recv()
@@ -452,17 +503,22 @@
         letters, embf, st,
     )
     edges(0)
+    normed_and_mixed(0, st, nrm, mx, gain1[...], mix)
+
+    copies["rc", 0].wait_recv()
+    copies["rc", 2] = send(xr.at[m], xr.at[m], one, 18, (j, sibling))
+    copies["rc", 1].wait_recv()
+    copies["rc", 3] = send(xr.at[across], xr.at[across], one, 19, (j, sibling))
+    copies["w_near"] = send(w_out, wo.at[m], one, 28, (j, sibling))
+    copies["w_far"] = send(w_out, wo.at[m], one, 29, (flipped, across))
     for copy in weights[:3]:
         copy.wait()
     strand(0)
     give_units(0)
 
-    own_rc.wait()
-    for k in range(1, n_mp):
-        copies["rc", k].wait_recv()
-    for k in range(n_mp):
-        copies["r_up", k].wait_recv()
-        copies["r_down", k].wait_recv()
+    copies["rc", 2].wait_recv()
+    copies["rc", 3].wait_recv()
+    edge_act(lambda copy: copy.wait_recv(), lambda copy: copy.wait())
     turn = jnp.where(
         iota2((ROWS, ROWS), 0) + iota2((ROWS, ROWS), 1) == ROWS - 1, 1.0, 0.0
     ).astype(BF16)
@@ -471,10 +527,11 @@
         3.0 - letters, embf, st,
     )
     edges(1)
+    normed_and_mixed(1, st, nrm, mx, gain1[...], mix)
     strand(1)
 
     give_units(1)
-    own_msg = fetch(msg.at[j], recv.at[j], 9)
+    own_msg = fetch(msg.at[j], recv.at[j], 19)
     copies["w_far"].wait_recv()
     copies["w_on"] = send(wo.at[across], wo.at[across], one, 30, (j, sibling))
 
@@ -487,7 +544,7 @@
     each(lambda d: to_unit(d).wait_recv())
     scanned(n_seq, j // (n_seq // 2), recv, ret, inside, give)
     each(lambda d: to_block(d).start())
-    own_ret = fetch(ret.at[j], states.at[j], 10)
+    own_ret = fetch(ret.at[j], states.at[j], 20)
     own_ret.wait()
     each(lambda d: to_block(d).wait_recv())
 
@@ -531,20 +588,20 @@
         both = dot(act[...], fv[:, lanes])
         return both[:ROWS] + both[ROWS:], lanes
 
-    for k in range(1, n_mp):
-        peer = mp_at(k)
+    for k, peer in enumerate((across, lax.rem(sibling + 2, n_mp), sibling)):
         value, _ = partial(peer)
-        part[k - 1] = value.astype(BF16)
-        copies["sum", k] = send(part.at[k - 1], got.at[k - 1], four, 5 + k, (j, peer))
+        part[k] = value.astype(BF16)
+        copies["sum", k] = send(part.at[k], got.at[k], four, 6 + k, (j, peer))
     value, lanes = partial(m)
     value = value + residual[:ROWS, lanes] + residual[ROWS:, lanes]
-    for k in range(1, n_mp):
+    for k in (2, 0, 1):
         copies["sum", k].wait_recv()
-        value = value + got[k - 1].astype(F32)
+        value = value + got[k].astype(F32)
     out[...] = value.astype(BF16)
 
     for copy in copies.values():
         copy.wait_send()
+    edge_act(lambda copy: copy.wait_send(), None)
     each(lambda d: to_unit(d).wait_send())
     each(lambda d: to_block(d).wait_send())
 
@@ -556,15 +613,18 @@
         args[index] = args[index].reshape(1, -1)
     for index in (10, 13):
         args[index] = args[index].T
-    in_place = {1, 2, 7, 8, 9, 17, 18, 19}
     vmem = pltpu.VMEM
     dma = pltpu.SemaphoreType.DMA
     width = 2 * PAIR
     scratch = [
+        vmem((1, ROWS), jnp.int32), vmem((1, 1024), F32), vmem((1, 1024), F32),
+        vmem((5, 1024), F32), vmem((64, 1024), BF16), vmem((1, width), F32),
+        vmem((64, width), BF16), vmem((64, 1024), BF16), vmem((1, width), F32),
+        vmem((64, width), BF16), vmem((1, width), F32),
         vmem((1024, width), BF16), vmem((1024, width), BF16), vmem((1024, width), BF16),
         vmem((1024, 1024), BF16), vmem((1024, 1024), BF16), vmem((n_mp, width, 1024), BF16),
         vmem((n_mp, ROWS, width), BF16), vmem((n_mp, ROWS, width), BF16),
-        vmem((ROWS, width), BF16), vmem((n_mp, 4, width), F32),
+        vmem((n_mp, 4, width), F32),
         vmem((2, n_mp, 16, width), BF16), vmem((2, n_mp, 16, width), BF16),
         vmem((1, ROWS), jnp.int32), vmem((1, ROWS), jnp.int32),
         vmem((2, ROWS, 1024), BF16), vmem((144, 1024), F32), vmem((5, 2 * ROWS, 1024), BF16),
@@ -577,15 +637,15 @@
         vmem((n_mp, 2 * ROWS, width), BF16), vmem((2 * ROWS, 1024), F32),
         vmem((2 * ROWS, 1024), BF16), vmem((3, ROWS, width), BF16), vmem((3, ROWS, width), BF16),
         vmem((n_seq, 96, PAIR), F32),
-        dma((11,)), dma((32,)), dma((32,)), dma((n_seq,)), dma((n_seq,)),
+        dma((23,)), dma((32,)), dma((32,)), dma((n_seq,)), dma((n_seq,)),
         dma((n_seq,)), dma((n_seq,)), dma((9,)), dma((9,)),
     ]
     return pl.pallas_call(
         functools.partial(kernel, n_seq, n_mp),
         out_shape=jax.ShapeDtypeStruct((ROWS, width), BF16),
         in_specs=[
-            pl.BlockSpec(memory_space=pl.ANY if i in in_place else pltpu.VMEM)
-            for i in range(len(args))
+            pl.BlockSpec(memory_space=pl.ANY)
+            for _ in args
         ],
         out_specs=pl.BlockSpec(memory_space=pltpu.VMEM),
         scratch_shapes=scratch,

time: 65.5 us -> 62.8 us (0.959)
  Pallas kernels: 63.9 us -> 61.2 us
    pallas_call x1, Pallas kernels: 63.9 us -> 61.2 us  [on_device(): pl.pallas_call(functools.partial(kernel, n_seq, n_mp), out_shape=jax.Shap...]
where the time goes in v3:
time: 62.8 us; the launch traced here: 62.6 us
  Pallas kernels  61.2 us (97%)
  local copies, waits for them, and re-layouts  1.47 us (2%)
    pallas_call x1, Pallas kernels, on_device(): pl.pallas_call(functools.partial(kernel, n_seq, n_mp), out_shape=jax.Shap...  61.2 us
    unnamed x1, local copies, waits for them, and re-layouts  1.47 us

profile of v3, /device:TPU:1, one launch (start us, length us, event | category | flops | bytes accessed | tf_op | source)
XLA Modules:
  0.0 62.6 jit_solution(17369616277800695596)
XLA Ops:
  0.0 61.2 %shard_map.190 = bf16[128,256]{1,0:T(8,128)(2,1)} custom-call(s32[1,128]{1,0:T(1,128)} %bitcast.15, bf16[128,256]{1,0:T(8,128)(2,1)} %hidden_fwd.1, bf16[128,256]{1,0:T(8,128)(2,1)} %hidden_rc.1, f32[4,256]{1,0:T(4,128)} %embed.1, f32[1,1024]{1,0:T(1,128)} %bitcast.10, f32[1,1024]{1,0:T(1,128)} %bitcast.11, f32[5,1024]{1,0:T(8,128)} %mix_in.1, ...), custom_call_target="tpu_custom_call" | custom-call | tf_op jit(solution)/shard_map/pallas_call | solution.py:643
  61.2 1.5 %copy.22 = bf16[128,256]{1,0:T(8,128)(2,1)} copy(bf16[128,256]{1,0:T(8,128)(2,1)} %shard_map.190) | data formatting | bytes 131072

commit v4 on v3

--- a/solution.py
+++ b/solution.py
@@ -249,7 +249,7 @@
     start_map[pair] = (srd[pair] + read[:, PAIR:]).astype(BF16)
 
 
-def scanned(n_seq, backward, recv, ret, inside, give):
+def scanned(n_seq, backward, recv, ret, inside):
     def place(i):
         return i + backward * (n_seq - 1 - 2 * i)
 
@@ -456,11 +456,6 @@
             send_sem=ss2.at[d], recv_sem=rs2.at[d],
             device_id=(seq_at(d), m), device_id_type=MESH,
         )
-
-    def give(block):
-        @pl.when(block != j)
-        def _():
-            to_block(lax.rem(block - j + n_seq, n_seq)).start()
 
     def to_block(d):
         return pltpu.make_async_remote_copy(
@@ -510,7 +505,11 @@
     copies["rc", 1].wait_recv()
     copies["rc", 3] = send(xr.at[across], xr.at[across], one, 19, (j, sibling))
     copies["w_near"] = send(w_out, wo.at[m], one, 28, (j, sibling))
-    copies["w_far"] = send(w_out, wo.at[m], one, 29, (flipped, across))
+    for index, seq_to in enumerate((j, flipped)):
+        rows = pl.ds(index * ROWS, ROWS)
+        copies["w_far", index] = send(
+            w_out.at[rows], wo.at[m, rows], one, 29 + 2 * index, (seq_to, across)
+        )
     for copy in weights[:3]:
         copy.wait()
     strand(0)
@@ -532,17 +531,18 @@
 
     give_units(1)
     own_msg = fetch(msg.at[j], recv.at[j], 19)
-    copies["w_far"].wait_recv()
-    copies["w_on"] = send(wo.at[across], wo.at[across], one, 30, (j, sibling))
 
     def local_body(pair, carry):
         local_terms(pair, aik, uw, vv, srd, local, start_map)
         return carry
 
     lax.fori_loop(0, 8, local_body, None)
+    copies["w_far", 0].wait_recv()
+    copies["w_far", 1].wait_recv()
+    copies["w_on"] = send(wo.at[across], wo.at[across], one, 30, (j, sibling))
     own_msg.wait()
     each(lambda d: to_unit(d).wait_recv())
-    scanned(n_seq, j // (n_seq // 2), recv, ret, inside, give)
+    scanned(n_seq, j // (n_seq // 2), recv, ret, inside)
     each(lambda d: to_block(d).start())
     own_ret = fetch(ret.at[j], states.at[j], 20)
     own_ret.wait()

time: 62.8 us -> 61 us (0.971)
  Pallas kernels: 61.2 us -> 59.4 us
    pallas_call x1, Pallas kernels: 61.2 us -> 59.4 us  [on_device(): pl.pallas_call(functools.partial(kernel, n_seq, n_mp), out_shape=jax.Shap...]
where the time goes in v4:
time: 61 us; the launch traced here: 60.9 us
  Pallas kernels  59.4 us (97%)
  local copies, waits for them, and re-layouts  1.47 us (2%)
    pallas_call x1, Pallas kernels, on_device(): pl.pallas_call(functools.partial(kernel, n_seq, n_mp), out_shape=jax.Shap...  59.4 us
    unnamed x1, local copies, waits for them, and re-layouts  1.47 us

profile of v4, /device:TPU:1, one launch (start us, length us, event | category | flops | bytes accessed | tf_op | source)
XLA Modules:
  0.0 60.9 jit_solution(7733821777580719395)
XLA Ops:
  0.0 59.4 %shard_map.190 = bf16[128,256]{1,0:T(8,128)(2,1)} custom-call(s32[1,128]{1,0:T(1,128)} %bitcast.15, bf16[128,256]{1,0:T(8,128)(2,1)} %hidden_fwd.1, bf16[128,256]{1,0:T(8,128)(2,1)} %hidden_rc.1, f32[4,256]{1,0:T(4,128)} %embed.1, f32[1,1024]{1,0:T(1,128)} %bitcast.10, f32[1,1024]{1,0:T(1,128)} %bitcast.11, f32[5,1024]{1,0:T(8,128)} %mix_in.1, ...), custom_call_target="tpu_custom_call" | custom-call | tf_op jit(solution)/shard_map/pallas_call | solution.py:643
  59.4 1.5 %copy.22 = bf16[128,256]{1,0:T(8,128)(2,1)} copy(bf16[128,256]{1,0:T(8,128)(2,1)} %shard_map.190) | data formatting | bytes 131072

commit v5 on v4

--- a/solution.py
+++ b/solution.py
@@ -249,7 +249,7 @@
     start_map[pair] = (srd[pair] + read[:, PAIR:]).astype(BF16)
 
 
-def scanned(n_seq, backward, recv, ret, inside):
+def scanned(n_seq, backward, recv, ret, inside, arrive):
     def place(i):
         return i + backward * (n_seq - 1 - 2 * i)
 
@@ -267,13 +267,14 @@
         full = jnp.concatenate([mapping.astype(BF16), blank], axis=0)
         return dot(state.astype(BF16), full)
 
-    for k in range(size):
-        for g in range(groups):
-            new = block(g * size + k)
-            if k:
-                so_far = inside[g * size + k - 1]
-                new = so_far + new + through(so_far, new[:HEAD])
-            inside[g * size + k] = new
+    def combine(first, last):
+        for k in range(size):
+            for g in range(first, last):
+                new = block(g * size + k)
+                if k:
+                    so_far = inside[g * size + k - 1]
+                    new = so_far + new + through(so_far, new[:HEAD])
+                inside[g * size + k] = new
 
     def onward(g, state):
         whole = inside[g * size + size - 1]
@@ -286,7 +287,13 @@
 
         return state + whole[HEAD:] + through(state, whole[:HEAD])
 
-    lax.fori_loop(0, groups, onward, jnp.zeros((32, PAIR), F32))
+    half = groups // 2
+    arrive(True)
+    combine(0, half)
+    state = lax.fori_loop(0, half, onward, jnp.zeros((32, PAIR), F32))
+    arrive(False)
+    combine(half, groups)
+    lax.fori_loop(half, groups, onward, state)
 
 
 def incoming(pair, states):
@@ -541,8 +548,18 @@
     copies["w_far", 1].wait_recv()
     copies["w_on"] = send(wo.at[across], wo.at[across], one, 30, (j, sibling))
     own_msg.wait()
-    each(lambda d: to_unit(d).wait_recv())
-    scanned(n_seq, j // (n_seq // 2), recv, ret, inside)
+
+    def arrive(near):
+        def wait(d):
+            apart = lax.rem(seq_at(-d) // (n_seq // 2) + j // (n_seq // 2), 2)
+
+            @pl.when(apart == int(not near))
+            def _():
+                to_unit(d).wait_recv()
+
+        each(wait)
+
+    scanned(n_seq, j // (n_seq // 2), recv, ret, inside, arrive)
     each(lambda d: to_block(d).start())
     own_ret = fetch(ret.at[j], states.at[j], 20)
     own_ret.wait()

time: 61 us -> 60.6 us (level)
  no operation moved by 1% of the time
where the time goes in v5:
time: 60.6 us; the launch traced here: 60.5 us
  Pallas kernels  59 us (97%)
  local copies, waits for them, and re-layouts  1.47 us (2%)
    pallas_call x1, Pallas kernels, on_device(): pl.pallas_call(functools.partial(kernel, n_seq, n_mp), out_shape=jax.Shap...  59 us
    unnamed x1, local copies, waits for them, and re-layouts  1.47 us

profile of v5, /device:TPU:1, one launch (start us, length us, event | category | flops | bytes accessed | tf_op | source)
XLA Modules:
  0.0 60.5 jit_solution(7523305508816548287)
XLA Ops:
  0.0 59.0 %shard_map.190 = bf16[128,256]{1,0:T(8,128)(2,1)} custom-call(s32[1,128]{1,0:T(1,128)} %bitcast.15, bf16[128,256]{1,0:T(8,128)(2,1)} %hidden_fwd.1, bf16[128,256]{1,0:T(8,128)(2,1)} %hidden_rc.1, f32[4,256]{1,0:T(4,128)} %embed.1, f32[1,1024]{1,0:T(1,128)} %bitcast.10, f32[1,1024]{1,0:T(1,128)} %bitcast.11, f32[5,1024]{1,0:T(8,128)} %mix_in.1, ...), custom_call_target="tpu_custom_call" | custom-call | tf_op jit(solution)/shard_map/pallas_call | solution.py:660
  59.0 1.5 %copy.22 = bf16[128,256]{1,0:T(8,128)(2,1)} copy(bf16[128,256]{1,0:T(8,128)(2,1)} %shard_map.190) | data formatting | bytes 131072
